TPU v7x, 32 devices: a whole 2x2x4 slice. The times are simulated.
32 devices in a mesh: dp: 8 (over z, x), tensor: 4 (over y, core).
Axes of the slice: x: 2, y: 2, z: 4, core: 2. Of those that a mesh axis runs over, the one named last changes fastest.
Arguments:
- frames: bfloat16 [16, 800, 768], P('dp', 'tensor'), may hold values from -6 to 6
- cotangent: float32 [16, 800, 768], P('dp', 'tensor'), may hold values from -6 to 6
- lengths: int32 [16], P('dp'), may hold values from 100 to 780
- query_weight: bfloat16 [768, 768], P(None, 'tensor'), may hold values from -0.21875 to 0.21875
- query_bias: float32 [768], P('tensor'), may hold values from -3 to 3
- key_weight: bfloat16 [768, 768], P(None, 'tensor'), may hold values from -0.21875 to 0.21875
- value_weight: bfloat16 [768, 768], P(None, 'tensor'), may hold values from -0.21875 to 0.21875
- value_bias: float32 [768], P('tensor'), may hold values from -3 to 3
- out_weight: bfloat16 [768, 768], P('tensor'), may hold values from -1.75 to 1.75
- out_bias: float32 [768], replicated, may hold values from -3 to 3
- first_gain: float32 [768], replicated, may hold values from 0.5 to 1.5
- first_shift: float32 [768], replicated, may hold values from -3 to 3
- up_weight: bfloat16 [768, 3072], P(None, 'tensor'), may hold values from -0.21875 to 0.21875
- up_bias: float32 [3072], P('tensor'), may hold values from -3 to 3
- down_weight: bfloat16 [3072, 768], P('tensor'), may hold values from -0.109375 to 0.109375
- down_bias: float32 [768], replicated, may hold values from -3 to 3
- second_gain: float32 [768], replicated, may hold values from 0.5 to 1.5
- second_shift: float32 [768], replicated, may hold values from -3 to 3
Outputs:
- layer_output: bfloat16 [16, 800, 768], P('dp', 'tensor')
- input_gradient: float32 [16, 800, 768], P('dp', 'tensor')
- query_weight_gradient: float32 [768, 768], P(None, 'tensor')
- query_bias_gradient: float32 [768], P('tensor')
- key_weight_gradient: float32 [768, 768], P(None, 'tensor')
- value_weight_gradient: float32 [768, 768], P(None, 'tensor')
- value_bias_gradient: float32 [768], P('tensor')
- out_weight_gradient: float32 [768, 768], P('tensor')
- out_bias_gradient: float32 [768], replicated
- first_gain_gradient: float32 [768], replicated
- first_shift_gradient: float32 [768], replicated
- up_weight_gradient: float32 [768, 3072], P(None, 'tensor')
- up_bias_gradient: float32 [3072], P('tensor')
- down_weight_gradient: float32 [3072, 768], P('tensor')
- down_bias_gradient: float32 [768], replicated
- second_gain_gradient: float32 [768], replicated
- second_shift_gradient: float32 [768], replicated
All inputs are finite; a program needn't handle non-finite values.
Results may differ from a plain program's by a relative error of at most 0.019.
Values may be sent and summed in bfloat16 or wider, within the bound.
A program may use at most 192 MiB of HBM per device.

v0:
```python
import jax
import jax.numpy as jnp
from jax import lax
from jax.sharding import PartitionSpec as P

HEAD_DIM = 64


EPSILON = 1e-05
ROOT_HALF = 0.7071067811865476
INVERSE_ROOT_TAU = 0.3989422804014327


def norm_rows(rows, gain, shift):
    centred = rows - jnp.mean(rows, axis=-1, keepdims=True)
    inverse = lax.rsqrt(jnp.mean(centred * centred, axis=-1, keepdims=True) + EPSILON)
    normed = centred * inverse
    return (normed * gain + shift, normed, inverse)


def norm_back(grad_out, normed, inverse, gain):
    scaled = grad_out * gain
    grad_in = inverse * (
        scaled
        - jnp.mean(scaled, axis=-1, keepdims=True)
        - normed * jnp.mean(scaled * normed, axis=-1, keepdims=True)
    )
    return (grad_in, jnp.sum(grad_out * normed, axis=0), jnp.sum(grad_out, axis=0))


def add_terms(running, terms):
    if running is None:
        return terms
    return tuple((left + right for left, right in zip(running, terms)))


def head_split(matrix):
    return matrix.reshape(matrix.shape[0], matrix.shape[1] // HEAD_DIM, HEAD_DIM)


def masked_scores(queries, key_rows, key_mask):
    scores = jnp.einsum(
        "qhd,khd->hqk",
        head_split(queries),
        head_split(key_rows),
        preferred_element_type=jnp.float32,
    ) * HEAD_DIM ** (-0.5)
    return jnp.where(key_mask[None, None, :], scores, -1e30)


def layer_forward(local_frames, key_count, weights):
    (
        query_weight,
        query_bias,
        key_weight,
        value_weight,
        value_bias,
        out_weight,
        out_bias,
        first_gain,
        first_shift,
        up_weight,
        up_bias,
        down_weight,
        down_bias,
        second_gain,
        second_shift,
    ) = weights
    full_frames = lax.all_gather(local_frames, "tensor", axis=0, tiled=True)
    length = full_frames.shape[0]
    queries = (
        jnp.dot(full_frames, query_weight, preferred_element_type=jnp.float32) + query_bias
    ).astype(jnp.bfloat16)
    key_rows = jnp.dot(full_frames, key_weight, preferred_element_type=jnp.float32).astype(
        jnp.bfloat16
    )
    values = (
        jnp.dot(full_frames, value_weight, preferred_element_type=jnp.float32) + value_bias
    ).astype(jnp.bfloat16)
    key_mask = jnp.arange(length) < key_count
    scores = masked_scores(queries, key_rows, key_mask)
    row_top = jnp.max(scores, axis=-1, keepdims=True)
    exponent = jnp.exp(scores - row_top)
    row_total = jnp.sum(exponent, axis=-1, keepdims=True)
    attention = (exponent / row_total).astype(jnp.bfloat16)
    log_total = row_top + jnp.log(row_total)
    context = (
        jnp.einsum(
            "hqk,khd->qhd", attention, head_split(values), preferred_element_type=jnp.float32
        )
        .reshape(length, -1)
        .astype(jnp.bfloat16)
    )
    attended = lax.psum_scatter(
        jnp.dot(context, out_weight, preferred_element_type=jnp.float32).astype(jnp.bfloat16),
        "tensor",
        scatter_dimension=0,
        tiled=True,
    ).astype(jnp.float32)
    first, first_normed, first_inverse = norm_rows(
        local_frames.astype(jnp.float32) + attended + out_bias, first_gain, first_shift
    )
    first_full = lax.all_gather(first.astype(jnp.bfloat16), "tensor", axis=0, tiled=True)
    hidden = jnp.dot(first_full, up_weight, preferred_element_type=jnp.float32) + up_bias
    activated = jax.nn.gelu(hidden, approximate=False).astype(jnp.bfloat16)
    mixed = lax.psum_scatter(
        jnp.dot(activated, down_weight, preferred_element_type=jnp.float32).astype(jnp.bfloat16),
        "tensor",
        scatter_dimension=0,
        tiled=True,
    ).astype(jnp.float32)
    output, second_normed, second_inverse = norm_rows(
        first + mixed + down_bias, second_gain, second_shift
    )
    stored = (
        full_frames,
        queries,
        key_rows,
        values,
        key_mask,
        log_total,
        context,
        first_normed,
        first_inverse,
        first_full,
        hidden,
        activated,
        second_normed,
        second_inverse,
    )
    return (output, stored)


def ffn_backward(stored, grad_output, weights):
    (
        full_frames,
        queries,
        key_rows,
        values,
        key_mask,
        log_total,
        context,
        first_normed,
        first_inverse,
        first_full,
        hidden,
        activated,
        second_normed,
        second_inverse,
    ) = stored
    up_weight, down_weight, second_gain = (weights[9], weights[11], weights[13])
    grad_second, second_gain_term, second_shift_term = norm_back(
        grad_output, second_normed, second_inverse, second_gain
    )
    down_bias_term = jnp.sum(grad_second, axis=0)
    grad_mixed = lax.all_gather(grad_second.astype(jnp.bfloat16), "tensor", axis=0, tiled=True)
    grad_active = jnp.einsum(
        "rd,fd->rf", grad_mixed, down_weight, preferred_element_type=jnp.float32
    )
    gelu_slope = (
        0.5 * (1.0 + lax.erf(hidden * ROOT_HALF))
        + hidden * jnp.exp(-0.5 * hidden * hidden) * INVERSE_ROOT_TAU
    )
    grad_hidden = (grad_active * gelu_slope).astype(jnp.bfloat16)
    down_weight_term = jnp.einsum(
        "rf,rd->fd", activated, grad_mixed, preferred_element_type=jnp.float32
    )
    up_weight_term = jnp.einsum(
        "rd,rf->df", first_full, grad_hidden, preferred_element_type=jnp.float32
    )
    up_bias_term = jnp.sum(grad_hidden, axis=0, dtype=jnp.float32)
    grad_first = (
        lax.psum_scatter(
            jnp.einsum(
                "rf,df->rd", grad_hidden, up_weight, preferred_element_type=jnp.float32
            ).astype(jnp.bfloat16),
            "tensor",
            scatter_dimension=0,
            tiled=True,
        ).astype(jnp.float32)
        + grad_second
    )
    return (
        grad_first,
        (up_weight_term, up_bias_term, down_weight_term),
        (second_gain_term, second_shift_term, down_bias_term),
    )


def attention_backward(stored, grad_first, weights):
    (
        full_frames,
        queries,
        key_rows,
        values,
        key_mask,
        log_total,
        context,
        first_normed,
        first_inverse,
        first_full,
        hidden,
        activated,
        second_normed,
        second_inverse,
    ) = stored
    query_weight, key_weight, value_weight, out_weight, first_gain = (
        weights[0],
        weights[2],
        weights[3],
        weights[5],
        weights[7],
    )
    length = full_frames.shape[0]
    factor = HEAD_DIM ** (-0.5)
    grad_attn_in, first_gain_term, first_shift_term = norm_back(
        grad_first, first_normed, first_inverse, first_gain
    )
    out_bias_term = jnp.sum(grad_attn_in, axis=0)
    grad_attended = lax.all_gather(grad_attn_in.astype(jnp.bfloat16), "tensor", axis=0, tiled=True)
    grad_context = jnp.einsum(
        "rd,cd->rc", grad_attended, out_weight, preferred_element_type=jnp.float32
    ).astype(jnp.bfloat16)
    out_weight_term = jnp.einsum(
        "rc,rd->cd", context, grad_attended, preferred_element_type=jnp.float32
    )
    scores = masked_scores(queries, key_rows, key_mask)
    attention = jnp.exp(scores - log_total)
    context_heads = head_split(grad_context)
    grad_values = (
        jnp.einsum(
            "hqk,qhd->khd",
            attention.astype(jnp.bfloat16),
            context_heads,
            preferred_element_type=jnp.float32,
        )
        .reshape(length, -1)
        .astype(jnp.bfloat16)
    )
    grad_attention = jnp.einsum(
        "qhd,khd->hqk", context_heads, head_split(values), preferred_element_type=jnp.float32
    )
    grad_scores = (
        attention * (grad_attention - jnp.sum(attention * grad_attention, axis=-1, keepdims=True))
    ).astype(jnp.bfloat16)
    grad_queries = (
        (
            jnp.einsum(
                "hqk,khd->qhd",
                grad_scores,
                head_split(key_rows),
                preferred_element_type=jnp.float32,
            )
            * factor
        )
        .reshape(length, -1)
        .astype(jnp.bfloat16)
    )
    grad_keys = (
        (
            jnp.einsum(
                "hqk,qhd->khd", grad_scores, head_split(queries), preferred_element_type=jnp.float32
            )
            * factor
        )
        .reshape(length, -1)
        .astype(jnp.bfloat16)
    )
    query_weight_term = jnp.einsum(
        "rd,rc->dc", full_frames, grad_queries, preferred_element_type=jnp.float32
    )
    key_weight_term = jnp.einsum(
        "rd,rc->dc", full_frames, grad_keys, preferred_element_type=jnp.float32
    )
    value_weight_term = jnp.einsum(
        "rd,rc->dc", full_frames, grad_values, preferred_element_type=jnp.float32
    )
    query_bias_term = jnp.sum(grad_queries, axis=0, dtype=jnp.float32)
    value_bias_term = jnp.sum(grad_values, axis=0, dtype=jnp.float32)
    total = jnp.einsum("rc,dc->rd", grad_queries, query_weight, preferred_element_type=jnp.float32)
    total = total + jnp.einsum(
        "rc,dc->rd", grad_keys, key_weight, preferred_element_type=jnp.float32
    )
    grad_input = (
        lax.psum_scatter(
            (
                total
                + jnp.einsum(
                    "rc,dc->rd", grad_values, value_weight, preferred_element_type=jnp.float32
                )
            ).astype(jnp.bfloat16),
            "tensor",
            scatter_dimension=0,
            tiled=True,
        ).astype(jnp.float32)
        + grad_attn_in
    )
    return (
        grad_input,
        (
            query_weight_term,
            query_bias_term,
            key_weight_term,
            value_weight_term,
            value_bias_term,
            out_weight_term,
        ),
        (first_gain_term, first_shift_term, out_bias_term),
    )


def shards(
    frames,
    cotangent,
    lengths,
    query_weight,
    query_bias,
    key_weight,
    value_weight,
    value_bias,
    out_weight,
    out_bias,
    first_gain,
    first_shift,
    up_weight,
    up_bias,
    down_weight,
    down_bias,
    second_gain,
    second_shift,
):
    weights = (
        query_weight,
        query_bias,
        key_weight,
        value_weight,
        value_bias,
        out_weight,
        out_bias,
        first_gain,
        first_shift,
        up_weight,
        up_bias,
        down_weight,
        down_bias,
        second_gain,
        second_shift,
    )
    micro_count = frames.shape[0]
    share_rows = frames.shape[1]
    share_start = lax.axis_index("tensor") * share_rows
    outputs = []
    stored_list = []
    for micro_index in range(micro_count):
        output, stored = layer_forward(frames[micro_index], lengths[micro_index], weights)
        outputs.append(output.astype(jnp.bfloat16))
        stored_list.append(stored)
    attention_total = None
    ffn_total = None
    first_total = None
    second_total = None
    input_grads = []
    for micro_index in range(micro_count):
        stored = layer_forward(frames[micro_index], lengths[micro_index], weights)[1]
        live_rows = (jnp.arange(share_rows) + share_start < lengths[micro_index]).astype(
            jnp.float32
        )[:, None]
        grad_first, ffn_terms, second_terms = ffn_backward(
            stored, cotangent[micro_index] * live_rows, weights
        )
        ffn_total = add_terms(ffn_total, ffn_terms)
        second_total = add_terms(second_total, second_terms)
        grad_input, attention_terms, first_terms = attention_backward(stored, grad_first, weights)
        attention_total = add_terms(attention_total, attention_terms)
        first_total = add_terms(first_total, first_terms)
        input_grads.append(grad_input)
    (
        query_weight_sum,
        query_bias_sum,
        key_weight_sum,
        value_weight_sum,
        value_bias_sum,
        out_weight_sum,
    ) = attention_total
    up_weight_sum, up_bias_sum, down_weight_sum = ffn_total
    summed = lax.psum(
        (
            query_weight_sum,
            query_bias_sum,
            key_weight_sum,
            value_weight_sum,
            value_bias_sum,
            out_weight_sum,
            up_weight_sum,
            up_bias_sum,
            down_weight_sum,
        ),
        "dp",
    )
    attention_total = summed[:6]
    ffn_total = summed[6:]
    first_gain_sum, first_shift_sum, out_bias_sum = first_total
    second_gain_sum, second_shift_sum, down_bias_sum = second_total
    small_sums = lax.psum(
        (
            first_gain_sum,
            first_shift_sum,
            out_bias_sum,
            second_gain_sum,
            second_shift_sum,
            down_bias_sum,
        ),
        ("dp", "tensor"),
    )
    return (
        jnp.stack(outputs),
        jnp.stack(input_grads),
        attention_total[0],
        attention_total[1],
        attention_total[2],
        attention_total[3],
        attention_total[4],
        attention_total[5],
        small_sums[2],
        small_sums[0],
        small_sums[1],
        ffn_total[0],
        ffn_total[1],
        ffn_total[2],
        small_sums[5],
        small_sums[3],
        small_sums[4],
    )


def solution(mesh):
    return jax.shard_map(
        shards,
        mesh=mesh,
        in_specs=(
            P("dp", "tensor", None),
            P("dp", "tensor", None),
            P("dp"),
            P(None, "tensor"),
            P("tensor"),
            P(None, "tensor"),
            P(None, "tensor"),
            P("tensor"),
            P("tensor", None),
            P(),
            P(),
            P(),
            P(None, "tensor"),
            P("tensor"),
            P("tensor", None),
            P(),
            P(),
            P(),
        ),
        out_specs=(
            P("dp", "tensor", None),
            P("dp", "tensor", None),
            P(None, "tensor"),
            P("tensor"),
            P(None, "tensor"),
            P(None, "tensor"),
            P("tensor"),
            P("tensor", None),
            P(),
            P(),
            P(),
            P(None, "tensor"),
            P("tensor"),
            P("tensor", None),
            P(),
            P(),
            P(),
        ),
        check_vma=False,
    )
```

profile of v0, /device:TPU:0, one launch (start us, length us, event | category | flops | bytes accessed | tf_op | source)
XLA Modules:
  0.0 706.6 jit_solution(2240069534778307623)
XLA Ops:
  7.3 2.0 fusion.96
  12.7 17.9 %all-gather.23.cloned.1.call-done = bf16[1,800,768]{2,1,0:T(8,128)(2,1)} async-done(((bf16[1,200,768]{2,1,0:T(8,128)(2,1)}), bf16[1,800,768]{2,1,0:T(8,128)(2,1)}) %all-gather.23.cloned.1.call-update) | async-done | bytes 1228816 | tf_op jit(solution)/shard_map/all_gather | solution.py:69
  30.7 1.9 convolution_convert_fusion.9
  32.7 2.0 fusion.48
  34.7 1.7 fusion.98
  40.2 1.6 fusion.62
  42.5 1.6 convolution_convert_fusion.5
  44.5 6.1 all-gather.25.cloned.1.call-done
  50.6 2.0 fusion.50
  52.6 2.0 fusion.49
  55.3 1.7 fusion.99
  58.3 2.1 copy-done.1
  60.4 1.6 fusion.61
  62.7 1.6 convolution_convert_fusion.3
  64.3 15.5 %reduce-scatter.9.cloned.1.call-done = bf16[200,768]{1,0:T(8,128)(2,1)} async-done(((bf16[800,768]{1,0:T(8,128)(2,1)}), bf16[200,768]{1,0:T(8,128)(2,1)}) %reduce-scatter.9.cloned.1.call-update) | async-done | bytes 307216 | tf_op jit(solution)/shard_map/reduce_scatter | solution.py:94
  81.0 28.0 %reduce-scatter.13.cloned.1.call-done = bf16[200,768]{1,0:T(8,128)(2,1)} async-done(((bf16[800,768]{1,0:T(8,128)(2,1)}), bf16[200,768]{1,0:T(8,128)(2,1)}) %reduce-scatter.13.cloned.1.call-update) | async-done | bytes 307216 | tf_op jit(solution)/shard_map/reduce_scatter | solution.py:94
  111.7 2.1 fusion.80
  115.0 16.7 %all-gather.13.cloned.1.call-done = bf16[800,768]{1,0:T(8,128)(2,1)} async-done(((bf16[200,768]{1,0:T(8,128)(2,1)}), bf16[800,768]{1,0:T(8,128)(2,1)}) %all-gather.13.cloned.1.call-update) | async-done | bytes 1228816 | tf_op jit(solution)/shard_map/all_gather | solution.py:103
  131.8 3.9 fusion.100
  135.6 15.9 %all-gather.11.cloned.1.call-done = bf16[800,768]{1,0:T(8,128)(2,1)} async-done(((bf16[200,768]{1,0:T(8,128)(2,1)}), bf16[800,768]{1,0:T(8,128)(2,1)}) %all-gather.11.cloned.1.call-update) | async-done | bytes 1228816 | tf_op jit(solution)/shard_map/all_gather | solution.py:103
  151.5 13.6 %fusion.14 = (bf16[800,768]{1,0:T(8,128)(2,1)S(1)}, bf16[800,768]{1,0:T(8,128)(2,1)}, f32[800,768]{1,0:T(8,128)}) fusion(f32[768]{0:T(1024)S(1)} %copy-done.76, f32[800,768]{1,0:T(8,128)} %fusion.100, bf16[800,768]{1,0:T(8,128)(2,1)} %all-gather.11.cloned.1.call-done, bf16[768,768]{1,0:T(8,128)(2,1)S(1)} %copy-done), kind=kOutput, calls=%fused_computation.28 | convolution fusion | flops 1024819200 | bytes 9784320 | tf_op jit(solution)/shard_map/dot_general | solution.py:104
  166.2 2.2 convolution_convert_fusion.4
  168.4 3.8 convolution_convert_fusion.2
  173.6 20.9 %reduce-scatter.11.cloned.1.call-done = bf16[200,768]{1,0:T(8,128)(2,1)} async-done(((bf16[800,768]{1,0:T(8,128)(2,1)}), bf16[200,768]{1,0:T(8,128)(2,1)}) %reduce-scatter.11.cloned.1.call-update) | async-done | bytes 307216 | tf_op jit(solution)/shard_map/reduce_scatter | solution.py:106
  194.5 29.4 %reduce-scatter.15.cloned.1.call-done = bf16[200,768]{1,0:T(8,128)(2,1)} async-done(((bf16[800,768]{1,0:T(8,128)(2,1)}), bf16[200,768]{1,0:T(8,128)(2,1)}) %reduce-scatter.15.cloned.1.call-update) | async-done | bytes 307216 | tf_op jit(solution)/shard_map/reduce_scatter | solution.py:106
  223.9 1.8 fusion.94
  226.9 2.2 fusion.90
  230.1 17.0 %all-gather.15.cloned.1.call-done = bf16[800,768]{1,0:T(8,128)(2,1)} async-done(((bf16[200,768]{1,0:T(8,128)(2,1)}), bf16[800,768]{1,0:T(8,128)(2,1)}) %all-gather.15.cloned.1.call-update) | async-done | bytes 1228816 | tf_op jit(solution)/shard_map/all_gather | solution.py:156
  247.1 4.7 convert_reduce_fusion.1
  252.8 2.2 convolution_convert_fusion.1
  255.2 11.6 %all-gather.19.cloned.1.call-done = bf16[800,768]{1,0:T(8,128)(2,1)} async-done(((bf16[200,768]{1,0:T(8,128)(2,1)}), bf16[800,768]{1,0:T(8,128)(2,1)}) %all-gather.19.cloned.1.call-update) | async-done | bytes 1228816 | tf_op jit(solution)/shard_map/all_gather | solution.py:156
  266.8 4.7 convert_reduce_fusion
  272.6 2.2 convolution_convert_fusion
  274.8 21.3 %reduce-scatter.17.cloned.1.call-done = bf16[200,768]{1,0:T(8,128)(2,1)} async-done(((bf16[800,768]{1,0:T(8,128)(2,1)}), bf16[200,768]{1,0:T(8,128)(2,1)}) %reduce-scatter.17.cloned.1.call-update) | async-done | bytes 307216 | tf_op jit(solution)/shard_map/reduce_scatter | solution.py:173
  296.1 29.3 %reduce-scatter.21.cloned.1.call-done = bf16[200,768]{1,0:T(8,128)(2,1)} async-done(((bf16[800,768]{1,0:T(8,128)(2,1)}), bf16[200,768]{1,0:T(8,128)(2,1)}) %reduce-scatter.21.cloned.1.call-update) | async-done | bytes 307216 | tf_op jit(solution)/shard_map/reduce_scatter | solution.py:173
  325.3 2.8 multiply_reduce_fusion.5
  328.1 2.0 fusion.92
  331.9 3.3 fusion.107
  335.2 2.9 fusion.106
  338.1 2.9 convolution_add_fusion
  342.0 7.6 %all-gather.17.cloned.1.call-done = bf16[800,768]{1,0:T(8,128)(2,1)} async-done(((bf16[200,768]{1,0:T(8,128)(2,1)}), bf16[800,768]{1,0:T(8,128)(2,1)}) %all-gather.17.cloned.1.call-update) | async-done | bytes 1228816 | tf_op jit(solution)/shard_map/all_gather | solution.py:220
  349.7 1.9 convolution_convert_fusion.7
  351.6 8.5 %multiply_reduce_fusion.1 = (f32[3,800]{1,0:T(4,128)S(1)}, f32[3,800,800]{1,2,0:T(8,128)}) fusion(f32[3,800,800]{1,2,0:T(8,128)} %copy-done.2, f32[3,800]{1,0:T(4,128)S(1)} %log_add_fusion.1, bf16[800,3,64]{0,2,1:T(8,128)(2,1)S(1)} %bitcast.240, bf16[800,3,64]{0,2,1:T(8,128)(2,1)S(1)} %bitcast.247), kind=kOutput, calls=%fused_computation.4 | convolution fusion | flops 251517600 | bytes 15993600 | tf_op jit(solution)/shard_map/qhd,khd->hqk/dot_general | solution.py:240
  360.1 9.7 %multiply_convert_fusion.1 = bf16[3,800,800]{1,2,0:T(8,128)(2,1)} fusion(f32[3,800,800]{1,2,0:T(8,128)} %get-tuple-element.94, f32[3,800,800]{1,2,0:T(8,128)} %copy-done.2, f32[3,800]{1,0:T(4,128)S(1)} %get-tuple-element.93, f32[3,800]{1,0:T(4,128)S(1)} %log_add_fusion.1), kind=kLoop, calls=%fused_computation.3 | loop fusion | flops 7680000 | bytes 19219200 | tf_op jit(solution)/shard_map/convert_element_type | solution.py:245
  369.7 3.8 fusion.52
  374.5 1.5 convert_reduce_fusion.5
  376.6 5.6 convert_reduce_fusion.3
  382.2 1.6 add_convert_fusion.1
  384.1 1.9 convolution_convert_fusion.6
  386.1 8.5 %multiply_reduce_fusion = (f32[3,800]{1,0:T(4,128)S(1)}, f32[3,800,800]{1,2,0:T(8,128)}) fusion(f32[3,800,800]{1,2,0:T(8,128)} %copy-done.1, f32[3,800]{1,0:T(4,128)S(1)} %log_add_fusion, bf16[800,3,64]{0,2,1:T(8,128)(2,1)S(1)} %bitcast.242, bf16[800,3,64]{0,2,1:T(8,128)(2,1)S(1)} %bitcast.245), kind=kOutput, calls=%fused_computation.1 | convolution fusion | flops 251517600 | bytes 15993600 | tf_op jit(solution)/shard_map/qhd,khd->hqk/dot_general | solution.py:240
  394.5 9.5 %multiply_convert_fusion = bf16[3,800,800]{1,2,0:T(8,128)(2,1)} fusion(f32[3,800,800]{1,2,0:T(8,128)} %get-tuple-element.92, f32[3,800,800]{1,2,0:T(8,128)} %copy-done.1, f32[3,800]{1,0:T(4,128)S(1)} %get-tuple-element.91, f32[3,800]{1,0:T(4,128)S(1)} %log_add_fusion), kind=kLoop, calls=%fused_computation | loop fusion | flops 7680000 | bytes 19219200 | tf_op jit(solution)/shard_map/convert_element_type | solution.py:245
  404.1 3.9 convert_reduce_fusion.4
  409.0 3.7 fusion.54
  414.0 2.1 convert_reduce_fusion.2
  416.2 1.6 add_convert_fusion
  418.1 5.4 convolution_add_fusion.1
  434.1 42.4 %all-reduce = (f32[768]{0:T(1024)}, f32[768]{0:T(1024)}, f32[768]{0:T(1024)}, f32[768]{0:T(1024)}, f32[768]{0:T(1024)}, /*index=5*/f32[768]{0:T(1024)}) all-reduce(f32[768]{0:T(1024)S(1)} %add.431, f32[768]{0:T(1024)S(1)} %add.432, f32[768]{0:T(1024)S(1)} %add.433, ...), channel_id=1, replica_groups=mesh['dp'=8,'tensor'=4] {'dp','tensor'}, use_global_device_ids=true, to_apply=%region_42.43 | all-reduce | flops 4608 | bytes 36864 | tf_op jit(solution)/shard_map/psum | solution.py:404
  476.7 22.9 %all-reduce.1 = (f32[192]{0:T(256)}, f32[192]{0:T(256)}, f32[768]{0:T(1024)}) all-reduce(f32[192]{0:T(256)S(1)} %add.423, f32[192]{0:T(256)S(1)} %add.429, f32[768]{0:T(1024)S(1)} %add.435), channel_id=1, replica_groups=mesh['dp'=8,'tensor'=4] {'dp'}, use_global_device_ids=true, to_apply=%region_33.34 | all-reduce | flops 1152 | bytes 9216 | tf_op jit(solution)/shard_map/psum | solution.py:386
  502.9 186.1 %all-reduce.5.cloned.1.call-done = (f32[768,192]{0,1:T(8,128)}, f32[768,192]{0,1:T(8,128)}, f32[768,192]{0,1:T(8,128)}, f32[192,768]{1,0:T(8,128)}, f32[768,768]{1,0:T(8,128)}, /*index=5*/f32[768,768]{1,0:T(8,128)}) async-done(((f32[768,192]{0,1:T(8,128)}, f32[768,192]{0,1:T(8,128)}, f32[768,192]{0,1:T(8,128)}, f32[192,768]{1,0:T(8,128)}, f32[768,768]{1,0:T(8,128)}, /*index=5*/f32[768,768]{1,0:T(8,128)}), ...) | async-done | bytes 7077904 | tf_op jit(solution)/shard_map/psum | solution.py:386
  688.9 2.1 copy.57
  691.0 1.9 copy.58
  692.9 1.9 copy.59
  695.6 1.4 copy.61
  698.2 1.4 copy.62
  (273 shorter events, 45.7 us)
Async XLA Ops:
  7.2 124.6 %copy-start = (bf16[768,768]{1,0:T(8,128)(2,1)S(1)}, bf16[768,768]{1,0:T(8,128)(2,1)}, u32[]{:S(2)}) copy-start(bf16[768,768]{1,0:T(8,128)(2,1)} %param.30) | copy-start | bytes 3538948
  7.2 25.4 %copy-start.38 = (bf16[768,192]{0,1:T(8,128)(2,1)S(1)}, bf16[768,192]{0,1:T(8,128)(2,1)}, u32[]{:S(2)}) copy-start(bf16[768,192]{0,1:T(8,128)(2,1)} %param.21) | copy-start | bytes 884740
  7.2 25.4 %copy-start.77 = (f32[192]{0:T(256)S(1)}, f32[192]{0:T(256)}, u32[]{:S(2)}) copy-start(f32[192]{0:T(256)} %param.22) | copy-start | bytes 2308
  7.2 23.4 %all-gather.23.cloned.1.call-start = ((), (), s32[]{:S(2)}) async-start(), calls=%async_computation.22 | async-start | bytes 1536000 | tf_op jit(solution)/shard_map/all_gather | solution.py:69
  9.3 41.3 %all-gather.25.cloned.1.call-start = ((), (), s32[]{:S(2)}) async-start(), calls=%async_computation.23 | async-start | bytes 1536000 | tf_op jit(solution)/shard_map/all_gather | solution.py:69
  10.1 69.7 %reduce-scatter.9.cloned.1.call-start = ((), (), s32[]{:S(2)}) async-start(), calls=%async_computation.8 | async-start | bytes 1536000 | tf_op jit(solution)/shard_map/reduce_scatter | solution.py:94
  32.6 3.8 copy-start.22
  36.4 3.8 copy-start.2
  44.1 10.5 %copy-start.41 = (bf16[768,192]{0,1:T(8,128)(2,1)S(1)}, bf16[768,192]{0,1:T(8,128)(2,1)}, u32[]{:S(2)}) copy-start(bf16[768,192]{0,1:T(8,128)(2,1)} %param.23) | copy-start | bytes 884740
  44.2 64.9 %reduce-scatter.13.cloned.1.call-start = ((), (), s32[]{:S(2)}) async-start(), calls=%async_computation.11 | async-start | bytes 1536000 | tf_op jit(solution)/shard_map/reduce_scatter | solution.py:94
  50.6 4.1 copy-start.5
  52.6 4.4 copy-start.24
  54.7 3.6 copy-start.51
  57.0 3.3 copy-start.1
  62.0 17.8 %copy-start.4 = (bf16[2,200,768]{2,1,0:T(8,128)(2,1)S(1)}, bf16[2,200,768]{2,1,0:T(8,128)(2,1)}, u32[]{:S(2)}) copy-start(bf16[2,200,768]{2,1,0:T(8,128)(2,1)} %param.18) | copy-start | bytes 1843204
  62.0 17.8 %copy-start.55 = (f32[768]{0:T(1024)S(1)}, f32[768]{0:T(1024)}, u32[]{:S(2)}) copy-start(f32[768]{0:T(1024)} %param.27) | copy-start | bytes 9220
  62.7 49.0 %copy-start.56 = (f32[768]{0:T(1024)S(1)}, f32[768]{0:T(1024)}, u32[]{:S(2)}) copy-start(f32[768]{0:T(1024)} %param.28) | copy-start | bytes 9220
  62.7 49.0 %copy-start.57 = (f32[768]{0:T(1024)S(1)}, f32[768]{0:T(1024)}, u32[]{:S(2)}) copy-start(f32[768]{0:T(1024)} %param.29) | copy-start | bytes 9220
  64.3 67.5 %all-gather.13.cloned.1.call-start = ((), (), s32[]{:S(2)}) async-start(), calls=%async_computation.12 | async-start | bytes 1536000 | tf_op jit(solution)/shard_map/all_gather | solution.py:103
  79.8 31.9 %copy-start.9 = (bf16[200,768]{1,0:T(8,128)(2,1)S(1)}, bf16[200,768]{1,0:T(8,128)(2,1)}, u32[]{:S(2)}) copy-start(bf16[200,768]{1,0:T(8,128)(2,1)} %reduce-scatter.9.cloned.1.call-done) | copy-start | bytes 921604
  113.9 37.7 %all-gather.11.cloned.1.call-start = ((), (), s32[]{:S(2)}) async-start(), calls=%async_computation.9 | async-start | bytes 1536000 | tf_op jit(solution)/shard_map/all_gather | solution.py:103
  114.4 37.1 %copy-start.76 = (f32[768]{0:T(1024)S(1)}, f32[768]{0:T(1024)}, u32[]{:S(2)}) copy-start(f32[768]{0:T(1024)} %param.31) | copy-start | bytes 9220
  114.4 80.1 %reduce-scatter.11.cloned.1.call-start = ((), (), s32[]{:S(2)}) async-start(), calls=%async_computation.10 | async-start | bytes 1536000 | tf_op jit(solution)/shard_map/reduce_scatter | solution.py:106
  151.5 14.6 %copy-start.75 = (bf16[768,768]{1,0:T(8,128)(2,1)S(1)}, bf16[768,768]{1,0:T(8,128)(2,1)}, u32[]{:S(2)}) copy-start(bf16[768,768]{1,0:T(8,128)(2,1)} %param.32) | copy-start | bytes 3538948
  168.3 55.6 %reduce-scatter.15.cloned.1.call-start = ((), (), s32[]{:S(2)}) async-start(), calls=%async_computation.13 | async-start | bytes 1536000 | tf_op jit(solution)/shard_map/reduce_scatter | solution.py:106
  168.4 55.5 %copy-start.10 = (bf16[200,768]{1,0:T(8,128)(2,1)S(1)}, bf16[200,768]{1,0:T(8,128)(2,1)}, u32[]{:S(2)}) copy-start(bf16[200,768]{1,0:T(8,128)(2,1)} %reduce-scatter.13.cloned.1.call-done) | copy-start | bytes 921604
  168.4 55.5 %copy-start.69 = (f32[768]{0:T(1024)S(1)}, f32[768]{0:T(1024)}, u32[]{:S(2)}) copy-start(f32[768]{0:T(1024)} %param.33) | copy-start | bytes 9220
  172.3 53.9 %copy-start.61 = (f32[768]{0:T(1024)S(1)}, f32[768]{0:T(1024)}, u32[]{:S(2)}) copy-start(f32[768]{0:T(1024)} %param.34) | copy-start | bytes 9220
  172.3 74.8 %all-gather.15.cloned.1.call-start = ((), (), s32[]{:S(2)}) async-start(), calls=%async_computation.14 | async-start | bytes 1536000 | tf_op jit(solution)/shard_map/all_gather | solution.py:156
  229.2 37.6 %all-gather.19.cloned.1.call-start = ((), (), s32[]{:S(2)}) async-start(), calls=%async_computation.18 | async-start | bytes 1536000 | tf_op jit(solution)/shard_map/all_gather | solution.py:156
  230.0 66.0 %reduce-scatter.17.cloned.1.call-start = ((), (), s32[]{:S(2)}) async-start(), calls=%async_computation.15 | async-start | bytes 1536000 | tf_op jit(solution)/shard_map/reduce_scatter | solution.py:173
  255.0 70.3 %reduce-scatter.21.cloned.1.call-start = ((), (), s32[]{:S(2)}) async-start(), calls=%async_computation.19 | async-start | bytes 1536000 | tf_op jit(solution)/shard_map/reduce_scatter | solution.py:173
  274.8 74.9 %all-gather.17.cloned.1.call-start = ((), (), s32[]{:S(2)}) async-start(), calls=%async_computation.16 | async-start | bytes 1536000 | tf_op jit(solution)/shard_map/all_gather | solution.py:220
  296.1 32.0 %copy-start.36 = (bf16[200,768]{1,0:T(8,128)(2,1)S(1)}, bf16[200,768]{1,0:T(8,128)(2,1)}, u32[]{:S(2)}) copy-start(bf16[200,768]{1,0:T(8,128)(2,1)} %reduce-scatter.17.cloned.1.call-done) | copy-start | bytes 921604
  331.8 52.3 %all-gather.21.cloned.1.call-start = ((), (), s32[]{:S(2)}) async-start(), calls=%async_computation.20 | async-start | bytes 1536000 | tf_op jit(solution)/shard_map/all_gather | solution.py:220
  331.9 3.3 copy-start.73
  331.9 3.3 copy-start.83
  335.2 2.9 copy-start.74
  335.2 2.9 copy-start.79
  338.0 2.9 copy-start.11
  338.0 11.6 %copy-start.48 = (bf16[192,768]{1,0:T(8,128)(2,1)S(1)}, bf16[192,768]{1,0:T(8,128)(2,1)}, u32[]{:S(2)}) copy-start(bf16[192,768]{1,0:T(8,128)(2,1)} %param.26) | copy-start | bytes 884740
  341.0 10.6 %copy-start.54 = (bf16[800,192]{0,1:T(8,128)(2,1)S(1)}, bf16[800,192]{0,1:T(8,128)(2,1)}, u32[]{:S(2)}) copy-start(bf16[800,192]{0,1:T(8,128)(2,1)} %copy-done.53) | copy-start | bytes 921604
  341.8 157.8 %reduce-scatter.19.cloned.1.call-start = ((), (), s32[]{:S(2)}) async-start(), calls=%async_computation.17 | async-start | bytes 1536000 | tf_op jit(solution)/shard_map/reduce_scatter | solution.py:285
  360.1 9.7 %copy-start.27 = (bf16[800,192]{0,1:T(8,128)(2,1)S(1)}, bf16[800,192]{0,1:T(8,128)(2,1)}, u32[]{:S(2)}) copy-start(bf16[800,192]{0,1:T(8,128)(2,1)} %copy-done.26) | copy-start | bytes 921604
  369.7 3.8 copy-start.42
  369.7 4.3 copy-start.3
  376.5 5.6 copy-start.45
  383.8 116.9 %reduce-scatter.23.cloned.1.call-start = ((), (), s32[]{:S(2)}) async-start(), calls=%async_computation.21 | async-start | bytes 1536000 | tf_op jit(solution)/shard_map/reduce_scatter | solution.py:285
  394.5 9.6 %copy-start.21 = (bf16[800,192]{0,1:T(8,128)(2,1)S(1)}, bf16[800,192]{0,1:T(8,128)(2,1)}, u32[]{:S(2)}) copy-start(bf16[800,192]{0,1:T(8,128)(2,1)} %copy-done.20) | copy-start | bytes 921604
  394.5 13.5 %copy-start.40 = (bf16[768,192]{0,1:T(8,128)(2,1)S(1)}, bf16[768,192]{0,1:T(8,128)(2,1)}, u32[]{:S(2)}) copy-start(bf16[768,192]{0,1:T(8,128)(2,1)} %param.21) | copy-start | bytes 884740
  404.1 9.9 %slice-start = ((s8[8601600]{0:T(1024)(128)(4,1)}), s8[4194304]{0:T(1024)(128)(4,1)S(1)}, s32[]{:S(2)}) async-start(s8[8601600]{0:T(1024)(128)(4,1)} %bitcast.214), calls=%async_computation.25 | async-start | bytes 8388608
  404.1 9.9 %slice-start.1 = ((s8[8601600]{0:T(1024)(128)(4,1)}), s8[4194304]{0:T(1024)(128)(4,1)S(1)}, s32[]{:S(2)}) async-start(s8[8601600]{0:T(1024)(128)(4,1)} %bitcast.214), calls=%async_computation.26 | async-start | bytes 8388608
  409.0 4.4 copy-start.43
  409.0 5.0 slice-start.2
  417.8 271.1 %all-reduce.5.cloned.1.call-start = ((), (), s32[]{:S(2)}) async-start(), calls=%async_computation.24 | async-start | bytes 14155776 | tf_op jit(solution)/shard_map/psum | solution.py:386
  418.1 5.4 copy-start.29
  418.1 5.4 copy-start.32
  432.1 44.4 %copy-start.66 = (f32[3,64]{1,0:T(4,128)S(1)}, f32[3,64]{1,0:T(4,128)}, u32[]{:S(2)}) copy-start(f32[3,64]{1,0:T(4,128)} %get-tuple-element.99) | copy-start | bytes 2308
  432.1 44.4 %copy-start.68 = (f32[3,64]{1,0:T(4,128)S(1)}, f32[3,64]{1,0:T(4,128)}, u32[]{:S(2)}) copy-start(f32[3,64]{1,0:T(4,128)} %get-tuple-element.101) | copy-start | bytes 2308
  432.1 44.5 %copy-start.65 = (f32[3,64]{1,0:T(4,128)S(1)}, f32[3,64]{1,0:T(4,128)}, u32[]{:S(2)}) copy-start(f32[3,64]{1,0:T(4,128)} %get-tuple-element.95) | copy-start | bytes 2308
  432.1 44.5 %copy-start.67 = (f32[3,64]{1,0:T(4,128)S(1)}, f32[3,64]{1,0:T(4,128)}, u32[]{:S(2)}) copy-start(f32[3,64]{1,0:T(4,128)} %get-tuple-element.97) | copy-start | bytes 2308
  432.1 67.4 %copy-start.13 = (f32[200,768]{1,0:T(8,128)S(1)}, f32[200,768]{1,0:T(8,128)}, u32[]{:S(2)}) copy-start(f32[200,768]{1,0:T(8,128)} %copy-done.12) | copy-start | bytes 1843204
  688.9 5.9 copy-start.50
  688.9 6.7 copy-start.19
  (40 other events, 69.0 us)
Sparse Core Ops, SparseCore 0:
  10.2 20.4 all-gather.22
  32.8 17.7 all-gather.24
  53.7 26.0 reduce-scatter.8
  83.0 26.0 reduce-scatter.12
  114.0 17.7 all-gather.12
  133.7 17.7 all-gather.10
  168.5 26.0 reduce-scatter.10
  197.9 26.0 reduce-scatter.14
  229.3 17.7 all-gather.14
  249.1 17.7 all-gather.18
  270.0 26.0 reduce-scatter.16
  299.3 26.0 reduce-scatter.20
  331.9 17.7 all-gather.16
  351.7 17.7 all-gather.20
  383.9 26.0 reduce-scatter.18
  417.9 26.4 reduce-scatter.22
  450.5 238.3 all-reduce.4
where the time goes:
time: 713 us; the launch traced here: 707 us
  waiting for transfers between devices  425 us (60%)
  matrix products  125 us (18%)
  blocking collectives  65.3 us (9%)
  other arithmetic  46.6 us (7%)
  local copies, waits for them, and re-layouts  27.6 us (4%)
  between operations  15.5 us (2%)
    psum x1, waiting for transfers between devices, shards(): lax.psum((query_weight_sum, query_bias_sum, key_weight_sum, value_weight_...  186 us
    reduce_scatter x2, waiting for transfers between devices, ffn_backward(): lax.psum_scatter(jnp.einsum('rf,df->rd', grad_hidden, up_weight, preferre...  50.5 us
    reduce_scatter x2, waiting for transfers between devices, layer_forward(): lax.psum_scatter(jnp.dot(activated, down_weight, preferred_element_type=j...  50.3 us
    reduce_scatter x2, waiting for transfers between devices, layer_forward(): lax.psum_scatter(jnp.dot(context, out_weight, preferred_element_type=jnp....  43.5 us
    psum x1, blocking collectives, shards(): lax.psum((first_gain_sum, first_shift_sum, out_bias_sum, second_gain_sum,...  42.4 us
    all_gather x2, waiting for transfers between devices, layer_forward(): lax.all_gather(first.astype(jnp.bfloat16), 'tensor', axis=0, tiled=True)  32.6 us
    all_gather x2, waiting for transfers between devices, ffn_backward(): lax.all_gather(grad_second.astype(jnp.bfloat16), 'tensor', axis=0, tiled=...  28.6 us
    unnamed x180, local copies, waits for them, and re-layouts  24.1 us
  transfers between devices with their start and end apart: 17, of which 14 were waited for; matrix products, arithmetic and copies ran while one was open for 20% of the time, Pallas kernels for 0%

commit v1 on v0

--- a/solution.py
+++ b/solution.py
@@ -1,7 +1,130 @@
+import functools
+
 import jax
 import jax.numpy as jnp
 from jax import lax
+from jax.experimental import pallas as pl
+from jax.experimental.pallas import tpu as pltpu
 from jax.sharding import PartitionSpec as P
+
+MESH = pl.DeviceIdType.MESH
+
+
+def ring_place(index, count):
+    return jnp.where(index % 2 == 0, index // 2, count - 1 - index // 2)
+
+
+def ring_index(place, count):
+    return jnp.where(place < count // 2, 2 * place, 2 * (count - 1 - place) + 1)
+
+
+def grad_ring(count, parts, *refs):
+    own = refs[:parts]
+    full = refs[parts : 2 * parts]
+    first = refs[2 * parts : 3 * parts]
+    landed = refs[3 * parts : 4 * parts]
+    add_send, add_recv, share_send, share_recv, out_sem = refs[4 * parts : 4 * parts + 5]
+    shared = refs[4 * parts + 5 :]
+    tensor = lax.axis_index("tensor")
+    place = ring_place(lax.axis_index("dp"), count)
+    right = ring_index((place + 1) % count, count)
+    left = ring_index((place + count - 1) % count, count)
+    barrier = pltpu.get_barrier_semaphore()
+    for peer in (left, right):
+        pl.semaphore_signal(barrier, inc=1, device_id=(peer, tensor), device_id_type=MESH)
+    pl.semaphore_wait(barrier, 2)
+    steps = count - 1
+
+    def chunk(way, step):
+        shift = count - 1 - step if way == 0 else 1 + step
+        return (place + shift) % count
+
+    def add_copy(part, way, step):
+        source = first[part].at[way] if step == 0 else landed[part].at[way, step - 1]
+        return pltpu.make_async_remote_copy(
+            src_ref=source,
+            dst_ref=landed[part].at[way, step],
+            send_sem=add_send.at[part, way, step],
+            recv_sem=add_recv.at[part, way, step],
+            device_id=(right if way == 0 else left, tensor),
+            device_id_type=MESH,
+        )
+
+    def share_copy(part, way, step):
+        shift = count - step if way == 0 else step
+        slot = shared[part].at[(place + shift) % count, way]
+        return pltpu.make_async_remote_copy(
+            src_ref=slot,
+            dst_ref=slot,
+            send_sem=share_send.at[part, way, step],
+            recv_sem=share_recv.at[part, way, step],
+            device_id=(right if way == 0 else left, tensor),
+            device_id_type=MESH,
+        )
+
+    for part in range(parts):
+        for way in range(2):
+            first[part][way] = own[part][chunk(way, 0), way].astype(jnp.bfloat16)
+            add_copy(part, way, 0).start()
+    for step in range(steps):
+        for part in range(parts):
+            for way in range(2):
+                add_copy(part, way, step).wait_recv()
+                total = landed[part][way, step].astype(jnp.float32) + own[part][
+                    chunk(way, step + 1), way
+                ].astype(jnp.float32)
+                if step < steps - 1:
+                    landed[part][way, step] = total.astype(jnp.bfloat16)
+                    add_copy(part, way, step + 1).start()
+                else:
+                    shared[part][place, way] = total.astype(jnp.bfloat16)
+                    share_copy(part, way, 0).start()
+    for step in range(steps):
+        for part in range(parts):
+            for way in range(2):
+                share_copy(part, way, step).wait_recv()
+                if step < steps - 1:
+                    share_copy(part, way, step + 1).start()
+    for part in range(parts):
+        for way in range(2):
+            for step in range(steps):
+                add_copy(part, way, step).wait_send()
+                share_copy(part, way, step).wait_send()
+    outs = [pltpu.make_async_copy(shared[part], full[part], out_sem.at[part]) for part in range(parts)]
+    for copy in outs:
+        copy.start()
+    for copy in outs:
+        copy.wait()
+
+
+def ring_sum(grads, count):
+    rows = [grad.shape[0] // (2 * count) for grad in grads]
+    blocks = [
+        grad.reshape(count, 2, size, grad.shape[1]) for grad, size in zip(grads, rows)
+    ]
+    parts = len(blocks)
+    half = [jax.ShapeDtypeStruct(block.shape, jnp.bfloat16) for block in blocks]
+    summed = pl.pallas_call(
+        functools.partial(grad_ring, count, parts),
+        out_shape=half,
+        in_specs=[pl.BlockSpec(memory_space=pltpu.VMEM)] * parts,
+        out_specs=[pl.BlockSpec(memory_space=pl.ANY)] * parts,
+        scratch_shapes=[pltpu.VMEM(block.shape[1:], jnp.bfloat16) for block in blocks]
+        + [
+            pltpu.VMEM((2, count - 1) + block.shape[2:], jnp.bfloat16) for block in blocks
+        ]
+        + [pltpu.SemaphoreType.DMA((parts, 2, count - 1))] * 4
+        + [pltpu.SemaphoreType.DMA((parts,))]
+        + [pltpu.VMEM(block.shape, jnp.bfloat16) for block in blocks],
+        compiler_params=pltpu.CompilerParams(
+            collective_id=0, has_side_effects=True, vmem_limit_bytes=60 << 20
+        ),
+        name="grad_ring",
+    )(*blocks)
+    return [
+        block.reshape(grad.shape).astype(jnp.float32) for block, grad in zip(summed, grads)
+    ]
+
 
 HEAD_DIM = 64
 
@@ -383,20 +506,18 @@
         out_weight_sum,
     ) = attention_total
     up_weight_sum, up_bias_sum, down_weight_sum = ffn_total
-    summed = lax.psum(
-        (
-            query_weight_sum,
-            query_bias_sum,
-            key_weight_sum,
-            value_weight_sum,
-            value_bias_sum,
-            out_weight_sum,
-            up_weight_sum,
-            up_bias_sum,
-            down_weight_sum,
-        ),
-        "dp",
-    )
+    count = lax.axis_size("dp")
+    large = (query_weight_sum, key_weight_sum, value_weight_sum, out_weight_sum, up_weight_sum, down_weight_sum)
+    if count % 2 == 0 and all(grad.shape[0] % (16 * count) == 0 for grad in large[:3]):
+        out_pad = jnp.pad(out_weight_sum, ((0, 256 - out_weight_sum.shape[0]), (0, 0)))
+        large = ring_sum(large[:3] + (out_pad,) + large[4:], count)
+        large[3] = large[3][: out_weight_sum.shape[0]]
+    else:
+        large = lax.psum(large, "dp")
+    query_bias_sum, value_bias_sum, up_bias_sum = lax.psum(
+        (query_bias_sum, value_bias_sum, up_bias_sum), "dp"
+    )
+    summed = (large[0], query_bias_sum, large[1], large[2], value_bias_sum, large[3], large[4], up_bias_sum, large[5])
     attention_total = summed[:6]
     ffn_total = summed[6:]
     first_gain_sum, first_shift_sum, out_bias_sum = first_total

time: 713 us -> 609 us (0.85)
  waiting for transfers between devices: 425 us -> 231 us
  Pallas kernels: 0 us -> 86.1 us
  other arithmetic: 46.6 us -> 55 us
    psum x1 -> x0, waiting for transfers between devices: 186 us -> none  [shards(): lax.psum((query_weight_sum, query_bias_sum, key_weight_sum, value_weight_...]
    pallas_call x0 -> x1, Pallas kernels: none -> 86.1 us  [ring_sum(): pl.pallas_call(functools.partial(grad_ring, count, parts), out_shape=half...]
    unnamed x180 -> x145, local copies, waits for them, and re-layouts: 24.1 us -> 14.6 us
    all_gather x2, waiting for transfers between devices: 7.66 us -> 0.01 us  [attention_backward(): lax.all_gather(grad_attn_in.astype(jnp.bfloat16), 'tensor', axis=0, tiled...]
  transfers between devices with their start and end apart: 17 -> 16, of which waited for: 14 -> 12; matrix products, arithmetic and copies ran while one was open for 20% -> 23% of each run, Pallas kernels for 0% -> 14%
where the time goes in v1:
time: 609 us; the launch traced here: 602 us
  waiting for transfers between devices  231 us (38%)
  matrix products  127 us (21%)
  Pallas kernels  86.1 us (14%)
  blocking collectives  60.3 us (10%)
  other arithmetic  55 us (9%)
  local copies, waits for them, and re-layouts  25.7 us (4%)
  between operations  15.2 us (2%)
    pallas_call x1, Pallas kernels, ring_sum(): pl.pallas_call(functools.partial(grad_ring, count, parts), out_shape=half...  86.1 us
    reduce_scatter x2, waiting for transfers between devices, ffn_backward(): lax.psum_scatter(jnp.einsum('rf,df->rd', grad_hidden, up_weight, preferre...  51 us
    reduce_scatter x2, waiting for transfers between devices, layer_forward(): lax.psum_scatter(jnp.dot(activated, down_weight, preferred_element_type=j...  50.3 us
    reduce_scatter x2, waiting for transfers between devices, layer_forward(): lax.psum_scatter(jnp.dot(context, out_weight, preferred_element_type=jnp....  43.4 us
    psum x1, blocking collectives, shards(): lax.psum((first_gain_sum, first_shift_sum, out_bias_sum, second_gain_sum,...  40 us
    all_gather x2, waiting for transfers between devices, layer_forward(): lax.all_gather(first.astype(jnp.bfloat16), 'tensor', axis=0, tiled=True)  33 us
    all_gather x2, waiting for transfers between devices, ffn_backward(): lax.all_gather(grad_second.astype(jnp.bfloat16), 'tensor', axis=0, tiled=...  27.9 us
    all_gather x2, waiting for transfers between devices, layer_forward(): full_frames = lax.all_gather(local_frames, 'tensor', axis=0, tiled=True)  24.1 us
  transfers between devices with their start and end apart: 16, of which 12 were waited for; matrix products, arithmetic and copies ran while one was open for 23% of the time, Pallas kernels for 14%

profile of v1, /device:TPU:0, one launch (start us, length us, event | category | flops | bytes accessed | tf_op | source)
XLA Modules:
  0.0 602.4 jit_solution(1935042175500316956)
XLA Ops:
  7.3 2.0 fusion.96
  12.7 17.9 %all-gather.23.cloned.1.call-done = bf16[1,800,768]{2,1,0:T(8,128)(2,1)} async-done(((bf16[1,200,768]{2,1,0:T(8,128)(2,1)}), bf16[1,800,768]{2,1,0:T(8,128)(2,1)}) %all-gather.23.cloned.1.call-update) | async-done | bytes 1228816 | tf_op jit(solution)/shard_map/all_gather | solution.py:192
  30.7 1.9 convolution_convert_fusion.9
  32.7 2.0 fusion.48
  34.7 1.7 fusion.98
  40.2 1.6 fusion.62
  42.6 1.6 convolution_convert_fusion.5
  44.4 6.2 %all-gather.25.cloned.1.call-done = bf16[1,800,768]{2,1,0:T(8,128)(2,1)} async-done(((bf16[1,200,768]{2,1,0:T(8,128)(2,1)}), bf16[1,800,768]{2,1,0:T(8,128)(2,1)}) %all-gather.25.cloned.1.call-update) | async-done | bytes 1228816 | tf_op jit(solution)/shard_map/all_gather | solution.py:192
  50.6 2.0 fusion.50
  52.6 2.0 fusion.49
  55.3 1.7 fusion.99
  58.3 2.2 copy-done.1
  60.5 1.6 fusion.61
  64.4 15.4 %reduce-scatter.9.cloned.1.call-done = bf16[200,768]{1,0:T(8,128)(2,1)} async-done(((bf16[800,768]{1,0:T(8,128)(2,1)}), bf16[200,768]{1,0:T(8,128)(2,1)}) %reduce-scatter.9.cloned.1.call-update) | async-done | bytes 307216 | tf_op jit(solution)/shard_map/reduce_scatter | solution.py:217
  81.0 28.0 %reduce-scatter.13.cloned.1.call-done = bf16[200,768]{1,0:T(8,128)(2,1)} async-done(((bf16[800,768]{1,0:T(8,128)(2,1)}), bf16[200,768]{1,0:T(8,128)(2,1)}) %reduce-scatter.13.cloned.1.call-update) | async-done | bytes 307216 | tf_op jit(solution)/shard_map/reduce_scatter | solution.py:217
  111.7 2.1 fusion.80
  114.7 17.0 %all-gather.13.cloned.1.call-done = bf16[800,768]{1,0:T(8,128)(2,1)} async-done(((bf16[200,768]{1,0:T(8,128)(2,1)}), bf16[800,768]{1,0:T(8,128)(2,1)}) %all-gather.13.cloned.1.call-update) | async-done | bytes 1228816 | tf_op jit(solution)/shard_map/all_gather | solution.py:226
  131.8 3.8 fusion.100
  135.6 15.9 %all-gather.11.cloned.1.call-done = bf16[800,768]{1,0:T(8,128)(2,1)} async-done(((bf16[200,768]{1,0:T(8,128)(2,1)}), bf16[800,768]{1,0:T(8,128)(2,1)}) %all-gather.11.cloned.1.call-update) | async-done | bytes 1228816 | tf_op jit(solution)/shard_map/all_gather | solution.py:226
  151.5 13.6 %fusion.14 = (bf16[800,768]{1,0:T(8,128)(2,1)S(1)}, bf16[800,768]{1,0:T(8,128)(2,1)}, f32[800,768]{1,0:T(8,128)}) fusion(f32[768]{0:T(1024)S(1)} %copy-done.62, f32[800,768]{1,0:T(8,128)} %fusion.100, bf16[800,768]{1,0:T(8,128)(2,1)} %all-gather.11.cloned.1.call-done, bf16[768,768]{1,0:T(8,128)(2,1)S(1)} %copy-done), kind=kOutput, calls=%fused_computation.28 | convolution fusion | flops 1024819200 | bytes 9784320 | tf_op jit(solution)/shard_map/dot_general | solution.py:227
  166.2 2.2 convolution_convert_fusion.4
  168.4 3.8 convolution_convert_fusion.2
  173.6 20.9 %reduce-scatter.11.cloned.1.call-done = bf16[200,768]{1,0:T(8,128)(2,1)} async-done(((bf16[800,768]{1,0:T(8,128)(2,1)}), bf16[200,768]{1,0:T(8,128)(2,1)}) %reduce-scatter.11.cloned.1.call-update) | async-done | bytes 307216 | tf_op jit(solution)/shard_map/reduce_scatter | solution.py:229
  194.6 29.4 %reduce-scatter.15.cloned.1.call-done = bf16[200,768]{1,0:T(8,128)(2,1)} async-done(((bf16[800,768]{1,0:T(8,128)(2,1)}), bf16[200,768]{1,0:T(8,128)(2,1)}) %reduce-scatter.15.cloned.1.call-update) | async-done | bytes 307216 | tf_op jit(solution)/shard_map/reduce_scatter | solution.py:229
  224.0 1.9 fusion.94
  227.1 1.9 fusion.90
  229.0 1.8 convert_element_type.361
  230.9 15.9 %all-gather.15.cloned.1.call-done = bf16[800,768]{1,0:T(8,128)(2,1)} async-done(((bf16[200,768]{1,0:T(8,128)(2,1)}), bf16[800,768]{1,0:T(8,128)(2,1)}) %all-gather.15.cloned.1.call-update) | async-done | bytes 1228816 | tf_op jit(solution)/shard_map/all_gather | solution.py:279
  246.8 4.1 convert_reduce_fusion.1
  252.0 2.2 convolution_convert_fusion.1
  254.7 11.9 %all-gather.19.cloned.1.call-done = bf16[800,768]{1,0:T(8,128)(2,1)} async-done(((bf16[200,768]{1,0:T(8,128)(2,1)}), bf16[800,768]{1,0:T(8,128)(2,1)}) %all-gather.19.cloned.1.call-update) | async-done | bytes 1228816 | tf_op jit(solution)/shard_map/all_gather | solution.py:279
  266.6 4.1 convert_reduce_fusion
  271.8 2.2 convolution_convert_fusion
  274.1 21.8 %reduce-scatter.17.cloned.1.call-done = bf16[200,768]{1,0:T(8,128)(2,1)} async-done(((bf16[800,768]{1,0:T(8,128)(2,1)}), bf16[200,768]{1,0:T(8,128)(2,1)}) %reduce-scatter.17.cloned.1.call-update) | async-done | bytes 307216 | tf_op jit(solution)/shard_map/reduce_scatter | solution.py:296
  295.8 29.3 %reduce-scatter.21.cloned.1.call-done = bf16[200,768]{1,0:T(8,128)(2,1)} async-done(((bf16[800,768]{1,0:T(8,128)(2,1)}), bf16[200,768]{1,0:T(8,128)(2,1)}) %reduce-scatter.21.cloned.1.call-update) | async-done | bytes 307216 | tf_op jit(solution)/shard_map/reduce_scatter | solution.py:296
  325.1 2.5 multiply_reduce_fusion.5
  330.9 1.9 pad_maximum_fusion.1
  332.8 3.3 fusion.107
  337.9 2.9 convolution_add_fusion
  340.8 2.9 convolution_add_fusion.1
  344.6 40.0 %all-reduce.1 = (f32[768]{0:T(1024)}, f32[768]{0:T(1024)}, f32[768]{0:T(1024)}, f32[768]{0:T(1024)}, f32[768]{0:T(1024)}, /*index=5*/f32[768]{0:T(1024)}) all-reduce(f32[768]{0:T(1024)S(1)} %add.423, f32[768]{0:T(1024)S(1)} %add.424, f32[768]{0:T(1024)S(1)} %add.425, ...), channel_id=1, replica_groups=mesh['dp'=8,'tensor'=4] {'dp','tensor'}, use_global_device_ids=true, to_apply=%region_38.39 | all-reduce | flops 4608 | bytes 36864 | tf_op jit(solution)/shard_map/psum | solution.py:525
  384.6 1.9 convolution_convert_fusion.7
  386.5 8.6 %multiply_reduce_fusion.1 = (f32[3,800]{1,0:T(4,128)S(1)}, f32[3,800,800]{1,2,0:T(8,128)}) fusion(f32[3,800,800]{1,2,0:T(8,128)} %copy-done.2, f32[3,800]{1,0:T(4,128)S(1)} %log_add_fusion.1, bf16[800,3,64]{0,2,1:T(8,128)(2,1)S(1)} %bitcast.268, bf16[800,3,64]{0,2,1:T(8,128)(2,1)} %bitcast.275), kind=kOutput, calls=%fused_computation.4 | convolution fusion | flops 251517600 | bytes 15993600 | tf_op jit(solution)/shard_map/qhd,khd->hqk/dot_general | solution.py:363
  395.2 9.5 %multiply_convert_fusion.1 = bf16[3,800,800]{1,2,0:T(8,128)(2,1)} fusion(f32[3,800,800]{1,2,0:T(8,128)} %get-tuple-element.117, f32[3,800,800]{1,2,0:T(8,128)} %copy-done.2, f32[3,800]{1,0:T(4,128)S(1)} %get-tuple-element.116, f32[3,800]{1,0:T(4,128)S(1)} %log_add_fusion.1), kind=kLoop, calls=%fused_computation.3 | loop fusion | flops 7680000 | bytes 19219200 | tf_op jit(solution)/shard_map/convert_element_type | solution.py:368
  404.7 4.5 fusion.52
  410.1 5.6 convert_reduce_fusion.3
  415.8 1.9 convolution_convert_fusion.6
  417.7 5.7 convert_reduce_fusion.2
  423.4 8.5 %multiply_reduce_fusion = (f32[3,800]{1,0:T(4,128)S(1)}, f32[3,800,800]{1,2,0:T(8,128)}) fusion(f32[3,800,800]{1,2,0:T(8,128)} %copy-done.1, f32[3,800]{1,0:T(4,128)S(1)} %log_add_fusion, bf16[800,3,64]{0,2,1:T(8,128)(2,1)S(1)} %bitcast.271, bf16[800,3,64]{0,2,1:T(8,128)(2,1)S(1)} %bitcast.273), kind=kOutput, calls=%fused_computation.1 | convolution fusion | flops 251517600 | bytes 15993600 | tf_op jit(solution)/shard_map/qhd,khd->hqk/dot_general | solution.py:363
  433.6 2.3 fusion.44
  435.8 2.3 copy.45
  438.1 1.7 fusion.102
  440.4 1.8 add_convert_fusion.1
  442.3 9.5 %multiply_convert_fusion = bf16[3,800,800]{1,2,0:T(8,128)(2,1)} fusion(f32[3,800,800]{1,2,0:T(8,128)} %get-tuple-element.115, f32[3,800,800]{1,2,0:T(8,128)} %copy-done.1, f32[3,800]{1,0:T(4,128)S(1)} %get-tuple-element.114, f32[3,800]{1,0:T(4,128)S(1)} %log_add_fusion), kind=kLoop, calls=%fused_computation | loop fusion | flops 7680000 | bytes 19219200 | tf_op jit(solution)/shard_map/convert_element_type | solution.py:368
  451.8 3.9 convert_reduce_fusion.4
  457.0 2.3 fusion.46
  459.3 2.3 copy.43
  462.1 3.8 fusion.54
  469.1 1.6 add_convert_fusion
  470.8 1.9 fusion.105
  474.1 86.1 %grad_ring.1 = (bf16[8,2,48,192]{3,2,1,0:T(8,128)(2,1)}, bf16[8,2,48,192]{3,2,1,0:T(8,128)(2,1)}, bf16[8,2,48,192]{3,2,1,0:T(8,128)(2,1)}, bf16[8,2,16,768]{3,2,...) custom-call(f32[8,2,48,192]{3,2,1,0:T(8,128)} %bitcast.244, ...), custom_call_target="tpu_custom_call" | custom-call | tf_op jit(solution)/shard_map/grad_ring/pallas_call | solution.py:107
  566.7 20.3 %all-reduce.2 = (f32[192]{0:T(256)}, f32[192]{0:T(256)}, f32[768]{0:T(1024)}) all-reduce(f32[192]{0:T(256)S(1)} %add.420, f32[192]{0:T(256)S(1)} %add.422, f32[768]{0:T(1024)S(1)} %add.426), channel_id=1, replica_groups=mesh['dp'=8,'tensor'=4] {'dp'}, use_global_device_ids=true, to_apply=%region_32.33 | all-reduce | flops 1152 | bytes 9216 | tf_op jit(solution)/shard_map/psum | solution.py:517
  587.8 2.8 bitcast_convert_fusion.1
  590.7 1.7 bitcast_convert_fusion
  (246 shorter events, 49.5 us)
Async XLA Ops:
  7.2 124.6 %copy-start = (bf16[768,768]{1,0:T(8,128)(2,1)S(1)}, bf16[768,768]{1,0:T(8,128)(2,1)}, u32[]{:S(2)}) copy-start(bf16[768,768]{1,0:T(8,128)(2,1)} %param.30) | copy-start | bytes 3538948
  7.2 25.4 %copy-start.36 = (bf16[768,192]{0,1:T(8,128)(2,1)S(1)}, bf16[768,192]{0,1:T(8,128)(2,1)}, u32[]{:S(2)}) copy-start(bf16[768,192]{0,1:T(8,128)(2,1)} %param.21) | copy-start | bytes 884740
  7.2 25.4 %copy-start.63 = (f32[192]{0:T(256)S(1)}, f32[192]{0:T(256)}, u32[]{:S(2)}) copy-start(f32[192]{0:T(256)} %param.22) | copy-start | bytes 2308
  7.2 23.4 %all-gather.23.cloned.1.call-start = ((), (), s32[]{:S(2)}) async-start(), calls=%async_computation.22 | async-start | bytes 1536000 | tf_op jit(solution)/shard_map/all_gather | solution.py:192
  9.3 41.3 %all-gather.25.cloned.1.call-start = ((), (), s32[]{:S(2)}) async-start(), calls=%async_computation.23 | async-start | bytes 1536000 | tf_op jit(solution)/shard_map/all_gather | solution.py:192
  10.1 69.7 %reduce-scatter.9.cloned.1.call-start = ((), (), s32[]{:S(2)}) async-start(), calls=%async_computation.8 | async-start | bytes 1536000 | tf_op jit(solution)/shard_map/reduce_scatter | solution.py:217
  32.6 3.8 copy-start.24
  36.4 3.8 copy-start.2
  36.4 2.2 copy-start.5
  36.5 2.5 copy-start.41
  36.5 2.5 copy-start.64
  39.6 2.3 copy-start.51
  40.2 2.4 copy-start.45
  44.2 10.5 %copy-start.39 = (bf16[768,192]{0,1:T(8,128)(2,1)S(1)}, bf16[768,192]{0,1:T(8,128)(2,1)}, u32[]{:S(2)}) copy-start(bf16[768,192]{0,1:T(8,128)(2,1)} %param.23) | copy-start | bytes 884740
  44.2 64.9 %reduce-scatter.13.cloned.1.call-start = ((), (), s32[]{:S(2)}) async-start(), calls=%async_computation.11 | async-start | bytes 1536000 | tf_op jit(solution)/shard_map/reduce_scatter | solution.py:217
  50.6 4.1 copy-start.6
  52.6 4.4 copy-start.26
  54.7 3.6 copy-start.49
  57.0 3.4 copy-start.1
  60.5 2.3 copy-start.46
  62.1 17.8 %copy-start.4 = (bf16[2,200,768]{2,1,0:T(8,128)(2,1)S(1)}, bf16[2,200,768]{2,1,0:T(8,128)(2,1)}, u32[]{:S(2)}) copy-start(bf16[2,200,768]{2,1,0:T(8,128)(2,1)} %param.18) | copy-start | bytes 1843204
  62.1 17.7 %copy-start.52 = (f32[768]{0:T(1024)S(1)}, f32[768]{0:T(1024)}, u32[]{:S(2)}) copy-start(f32[768]{0:T(1024)} %param.27) | copy-start | bytes 9220
  62.8 48.9 %copy-start.53 = (f32[768]{0:T(1024)S(1)}, f32[768]{0:T(1024)}, u32[]{:S(2)}) copy-start(f32[768]{0:T(1024)} %param.28) | copy-start | bytes 9220
  62.8 48.9 %copy-start.54 = (f32[768]{0:T(1024)S(1)}, f32[768]{0:T(1024)}, u32[]{:S(2)}) copy-start(f32[768]{0:T(1024)} %param.29) | copy-start | bytes 9220
  64.4 67.4 %all-gather.13.cloned.1.call-start = ((), (), s32[]{:S(2)}) async-start(), calls=%async_computation.12 | async-start | bytes 1536000 | tf_op jit(solution)/shard_map/all_gather | solution.py:226
  79.8 31.9 %copy-start.10 = (bf16[200,768]{1,0:T(8,128)(2,1)S(1)}, bf16[200,768]{1,0:T(8,128)(2,1)}, u32[]{:S(2)}) copy-start(bf16[200,768]{1,0:T(8,128)(2,1)} %reduce-scatter.9.cloned.1.call-done) | copy-start | bytes 921604
  113.9 37.7 %all-gather.11.cloned.1.call-start = ((), (), s32[]{:S(2)}) async-start(), calls=%async_computation.9 | async-start | bytes 1536000 | tf_op jit(solution)/shard_map/all_gather | solution.py:226
  114.4 37.1 %copy-start.62 = (f32[768]{0:T(1024)S(1)}, f32[768]{0:T(1024)}, u32[]{:S(2)}) copy-start(f32[768]{0:T(1024)} %param.31) | copy-start | bytes 9220
  114.5 80.1 %reduce-scatter.11.cloned.1.call-start = ((), (), s32[]{:S(2)}) async-start(), calls=%async_computation.10 | async-start | bytes 1536000 | tf_op jit(solution)/shard_map/reduce_scatter | solution.py:229
  151.5 14.7 %copy-start.61 = (bf16[768,768]{1,0:T(8,128)(2,1)S(1)}, bf16[768,768]{1,0:T(8,128)(2,1)}, u32[]{:S(2)}) copy-start(bf16[768,768]{1,0:T(8,128)(2,1)} %param.32) | copy-start | bytes 3538948
  168.4 55.6 %reduce-scatter.15.cloned.1.call-start = ((), (), s32[]{:S(2)}) async-start(), calls=%async_computation.13 | async-start | bytes 1536000 | tf_op jit(solution)/shard_map/reduce_scatter | solution.py:229
  168.4 55.5 %copy-start.56 = (f32[768]{0:T(1024)S(1)}, f32[768]{0:T(1024)}, u32[]{:S(2)}) copy-start(f32[768]{0:T(1024)} %param.33) | copy-start | bytes 9220
  172.3 54.0 %copy-start.55 = (f32[768]{0:T(1024)S(1)}, f32[768]{0:T(1024)}, u32[]{:S(2)}) copy-start(f32[768]{0:T(1024)} %param.34) | copy-start | bytes 9220
  172.3 74.6 %all-gather.15.cloned.1.call-start = ((), (), s32[]{:S(2)}) async-start(), calls=%async_computation.14 | async-start | bytes 1536000 | tf_op jit(solution)/shard_map/all_gather | solution.py:279
  224.0 2.4 copy-start.17
  229.0 37.6 %all-gather.19.cloned.1.call-start = ((), (), s32[]{:S(2)}) async-start(), calls=%async_computation.18 | async-start | bytes 1536000 | tf_op jit(solution)/shard_map/all_gather | solution.py:279
  230.9 65.0 %reduce-scatter.17.cloned.1.call-start = ((), (), s32[]{:S(2)}) async-start(), calls=%async_computation.15 | async-start | bytes 1536000 | tf_op jit(solution)/shard_map/reduce_scatter | solution.py:296
  254.2 70.9 %reduce-scatter.21.cloned.1.call-start = ((), (), s32[]{:S(2)}) async-start(), calls=%async_computation.19 | async-start | bytes 1536000 | tf_op jit(solution)/shard_map/reduce_scatter | solution.py:296
  274.0 110.6 %all-gather.17.cloned.1.call-start = ((), (), s32[]{:S(2)}) async-start(), calls=%async_computation.16 | async-start | bytes 1536000 | tf_op jit(solution)/shard_map/all_gather | solution.py:343
  325.1 2.6 copy-start.11
  325.1 2.6 copy-start.12
  325.1 2.6 copy-start.16
  325.1 2.6 copy-start.34
  325.1 2.6 copy-start.35
  330.8 85.0 %all-gather.21.cloned.1.call-start = ((), (), s32[]{:S(2)}) async-start(), calls=%async_computation.20 | async-start | bytes 1536000 | tf_op jit(solution)/shard_map/all_gather | solution.py:343
  332.8 3.3 copy-start.59
  332.8 3.3 copy-start.70
  337.9 2.9 copy-start.58
  337.9 2.9 copy-start.67
  340.8 2.9 copy-start.13
  340.8 43.8 %copy-start.47 = (bf16[192,768]{1,0:T(8,128)(2,1)S(1)}, bf16[192,768]{1,0:T(8,128)(2,1)}, u32[]{:S(2)}) copy-start(bf16[192,768]{1,0:T(8,128)(2,1)} %param.26) | copy-start | bytes 884740
  344.6 247.8 %reduce-scatter.19.cloned.1.call-start = ((), (), s32[]{:S(2)}) async-start(), calls=%async_computation.17 | async-start | bytes 1536000 | tf_op jit(solution)/shard_map/reduce_scatter | solution.py:408
  395.2 9.5 %copy-start.28 = (bf16[800,192]{0,1:T(8,128)(2,1)S(1)}, bf16[800,192]{0,1:T(8,128)(2,1)}, u32[]{:S(2)}) copy-start(bf16[800,192]{0,1:T(8,128)(2,1)} %copy-done.27) | copy-start | bytes 921604
  404.7 4.5 copy-start.3
  404.7 4.5 copy-start.25
  417.7 5.7 copy-start.50
  438.1 2.2 copy-start.20
  438.1 2.3 copy-start.42
  442.2 151.2 %reduce-scatter.23.cloned.1.call-start = ((), (), s32[]{:S(2)}) async-start(), calls=%async_computation.21 | async-start | bytes 1536000 | tf_op jit(solution)/shard_map/reduce_scatter | solution.py:408
  442.3 9.5 %copy-start.23 = (bf16[800,192]{0,1:T(8,128)(2,1)S(1)}, bf16[800,192]{0,1:T(8,128)(2,1)}, u32[]{:S(2)}) copy-start(bf16[800,192]{0,1:T(8,128)(2,1)} %copy-done.22) | copy-start | bytes 921604
  456.2 5.4 copy-start.21
  462.1 3.8 copy-start.9
  561.2 4.3 copy-start.48
  587.0 3.7 copy-start.44
  (23 other events, 32.6 us)
Sparse Core Ops, SparseCore 0:
  10.2 20.4 all-gather.22
  32.8 17.7 all-gather.24
  53.7 26.0 reduce-scatter.8
  83.0 26.0 reduce-scatter.12
  114.0 17.7 all-gather.12
  133.7 17.7 all-gather.10
  168.5 26.0 reduce-scatter.10
  197.9 26.0 reduce-scatter.14
  229.1 17.7 all-gather.14
  248.8 17.7 all-gather.18
  269.8 26.0 reduce-scatter.16
  299.0 26.0 reduce-scatter.20
  330.9 17.7 all-gather.16
  350.1 17.8 all-gather.20
  442.3 27.1 reduce-scatter.18
  472.8 26.0 reduce-scatter.22

commit v2 on v1

v2 whole, which is shorter than its diff:
```python
import functools

import jax
import jax.numpy as jnp
from jax import lax
from jax.experimental import pallas as pl
from jax.experimental.pallas import tpu as pltpu
from jax.sharding import PartitionSpec as P

MESH = pl.DeviceIdType.MESH
HEAD_DIM = 64
EPSILON = 1e-05
ROOT_HALF = 0.7071067811865476
INVERSE_ROOT_TAU = 0.3989422804014327
MASKED = -1e30
VMEM_BYTES = 62 << 20
BF = jnp.bfloat16
F32 = jnp.float32


def up_to(size, unit):
    return (size + unit - 1) // unit * unit


def dot(left, right):
    return jnp.dot(left, right, preferred_element_type=F32)


def dot_nt(left, right):
    return lax.dot_general(left, right, (((1,), (1,)), ((), ())), preferred_element_type=F32)


def dot_tn(left, right):
    return lax.dot_general(left, right, (((0,), (0,)), ((), ())), preferred_element_type=F32)


def pad_rows(rows, size):
    extra = size - rows.shape[0]
    if extra == 0:
        return rows
    return jnp.concatenate([rows, jnp.zeros((extra, rows.shape[1]), rows.dtype)], axis=0)


class Group:
    def __init__(self):
        self.dp = lax.axis_index("dp")
        self.own = lax.axis_index("tensor")
        self.y = self.own // 2
        self.core = self.own % 2
        self.mate = self.y * 2 + (1 - self.core)
        self.far = (1 - self.y) * 2 + self.core

    def greet(self):
        barrier = pltpu.get_barrier_semaphore()
        for peer in (self.mate, self.far):
            pl.semaphore_signal(barrier, inc=1, device_id=(self.dp, peer), device_id_type=MESH)
        pl.semaphore_wait(barrier, 2)

    def share(self, turn):
        late = turn // 2
        other = ((turn + 1) // 2) % 2
        ybit = (1 - self.y) * (1 - late) + self.y * late
        core = self.core * (1 - other) + (1 - self.core) * other
        return ybit * 2 + core

    def copy(self, source, target, send, recv, peer):
        return pltpu.make_async_remote_copy(
            src_ref=source,
            dst_ref=target,
            send_sem=send,
            recv_sem=recv,
            device_id=(self.dp, peer),
            device_id_type=MESH,
        )


class Gather:
    def __init__(self, group, full, send, recv):
        self.group, self.full, self.send, self.recv = group, full, send, recv

    def _copy(self, seq, kind):
        group = self.group
        share = group.far if kind == 2 else group.own
        slot = self.full.at[seq, share]
        peer = group.far if kind == 0 else group.mate
        return group.copy(slot, slot, self.send.at[seq, kind], self.recv.at[seq, kind], peer)

    def start(self, seq):
        self._copy(seq, 0).start()
        self._copy(seq, 1).start()

    def wait(self, seq, turn):
        @pl.when(turn == 0)
        def _():
            self._copy(seq, 0).wait_recv()
            self._copy(seq, 2).start()

        @pl.when(turn == 1)
        def _():
            self._copy(seq, 2).wait_recv()

        @pl.when(turn == 2)
        def _():
            self._copy(seq, 1).wait_recv()

    def close(self, seq):
        for kind in range(3):
            self._copy(seq, kind).wait_send()


class Scatter:
    def __init__(self, group, buffers, send, recv):
        self.group = group
        self.outgoing, self.keep, self.near, self.cross, self.landed = buffers
        self.send, self.recv = send, recv

    def _near(self, seq, index):
        return self.group.copy(
            self.outgoing.at[seq, index],
            self.near.at[seq, index],
            self.send.at[seq, index],
            self.recv.at[seq, index],
            self.group.mate,
        )

    def _cross(self, seq):
        return self.group.copy(
            self.cross.at[seq],
            self.landed.at[seq],
            self.send.at[seq, 2],
            self.recv.at[seq, 2],
            self.group.far,
        )

    def put(self, seq, turn, terms):
        @pl.when((turn == 0) | (turn == 3))
        def _():
            self.keep[seq, turn // 3] = terms

        @pl.when((turn == 1) | (turn == 2))
        def _():
            self.outgoing[seq, turn - 1] = terms.astype(BF)
            self._near(seq, turn - 1).start()

        @pl.when(turn == 2)
        def _():
            self._near(seq, 0).wait_recv()
            total = self.keep[seq, 0] + self.near[seq, 0].astype(F32)
            self.cross[seq] = total.astype(BF)
            self._cross(seq).start()

    def take(self, seq):
        self._near(seq, 1).wait_recv()
        self._cross(seq).wait_recv()
        for index in range(2):
            self._near(seq, index).wait_send()
        self._cross(seq).wait_send()
        return (
            self.keep[seq, 1]
            + self.near[seq, 1].astype(F32)
            + self.landed[seq].astype(F32)
        )


def norm(rows):
    centred = rows - jnp.mean(rows, axis=-1, keepdims=True)
    inverse = lax.rsqrt(jnp.mean(centred * centred, axis=-1, keepdims=True) + EPSILON)
    return centred * inverse, inverse


def norm_back(grad, normed, inverse, gain):
    scaled = grad * gain
    return inverse * (
        scaled
        - jnp.mean(scaled, axis=-1, keepdims=True)
        - normed * jnp.mean(scaled * normed, axis=-1, keepdims=True)
    )


def sum_rows(rows):
    return jnp.sum(rows, axis=0, keepdims=True)


def lane_index(rows, lanes):
    return lax.broadcasted_iota(jnp.int32, (rows, lanes), 1)


def front(
    lengths, frames, cotangent, query_weight, key_weight, value_weight, projection_bias,
    out_weight, up_weight, down_weight, vectors,
    layer_output, full_frames, projected, context, grad_attended, up_grad, down_grad, sums,
    wide_weight, wide_out, first_normed, first_inverse, first_full, hidden, activated,
    grad_second, grad_mixed, grad_hidden,
    outgoing, keep, near, cross, landed,
    gather_send, gather_recv, scatter_send, scatter_recv,
):
    seqs, share_rows, width = frames.shape
    rows = full_frames.shape[2]
    heads_width = query_weight.shape[1]
    lanes = wide_weight.shape[1] // 3
    heads = heads_width // HEAD_DIM
    length = 4 * rows
    group = Group()
    out_bias, first_gain, first_shift, down_bias, second_gain, second_shift, up_bias = (
        vectors[index : index + 1] for index in range(7)
    )
    buffers = (outgoing, keep, near, cross, landed)
    gathers = [
        Gather(group, full, gather_send.at[index], gather_recv.at[index])
        for index, full in enumerate((full_frames, first_full, grad_mixed))
    ]
    scatters = [
        Scatter(group, buffers, scatter_send.at[index], scatter_recv.at[index]) for index in range(3)
    ]

    group.greet()

    def each(stage):
        def body(seq, carry):
            stage(seq)
            return carry

        lax.fori_loop(0, seqs, body, 0)

    def turns(step):
        def body(turn, carry):
            step(turn)
            return carry

        lax.fori_loop(0, 4, body, 0)

    def send_frames(seq):
        full_frames[seq, group.own] = pad_rows(frames[seq].astype(F32), rows).astype(BF)
        gathers[0].start(seq)

    each(send_frames)
    wide_weight[...] = jnp.zeros_like(wide_weight)
    for index, weight in enumerate((query_weight, key_weight, value_weight)):
        wide_weight[:, index * lanes : index * lanes + heads_width] = weight[...]
    wide_out[...] = jnp.zeros_like(wide_out)
    wide_out[:heads_width] = out_weight[...]
    sums[...] = jnp.zeros_like(sums)
    up_grad[...] = jnp.zeros_like(up_grad)
    down_grad[...] = jnp.zeros_like(down_grad)

    def attention(seq):
        def project(step):
            turn = (1 - step // 2) * (3 - step) + (step // 2) * (step - 2)
            gathers[0].wait(seq, turn)
            share = group.share(turn)
            result = dot(full_frames[seq, share], wide_weight[...]) + projection_bias[...]
            place = lax.broadcasted_iota(jnp.int32, (rows, lanes), 0)
            dead = (place >= share_rows) | (place + share * share_rows >= lengths[seq])
            flag = jnp.where(dead & (lane_index(rows, lanes) == heads_width), MASKED, 0.0)
            start = pl.multiple_of(share * rows, 16)
            projected[seq, pl.ds(start, rows), 0:lanes] = (
                result[:, :lanes].astype(BF) * HEAD_DIM ** (-0.5)
            ).astype(BF)
            projected[seq, pl.ds(start, rows), lanes : 2 * lanes] = (
                result[:, lanes : 2 * lanes] + flag
            ).astype(BF)
            projected[seq, pl.ds(start, rows), 2 * lanes : 3 * lanes] = result[:, 2 * lanes :].astype(BF)

        turns(project)

        def attend(turn):
            share = group.share(turn)
            start = pl.multiple_of(share * rows, 16)
            queries = projected[seq, pl.ds(start, rows), 0:lanes]
            lane = lane_index(rows, lanes)
            mixed = jnp.zeros((rows, lanes), F32)
            for head in range(heads):
                inside = lane // HEAD_DIM == head
                picked = jnp.where(inside | (lane == heads_width), queries, jnp.zeros_like(queries))
                scores = dot_nt(picked, projected[seq, :, lanes : 2 * lanes])
                exponent = jnp.exp(scores - jnp.max(scores, axis=-1, keepdims=True))
                weights = exponent * (1.0 / jnp.sum(exponent, axis=-1, keepdims=True))
                part = dot(weights.astype(BF), projected[seq, :, 2 * lanes : 3 * lanes])
                mixed = jnp.where(inside, part, mixed)
            mixed = mixed.astype(BF)
            context[seq, pl.ds(start, rows)] = mixed
            scatters[0].put(seq, turn, dot(mixed, wide_out[...]))

        turns(attend)

    each(attention)

    def first_norm(seq):
        attended = scatters[0].take(seq)
        normed, inverse = norm(full_frames[seq, group.own].astype(F32) + attended + out_bias)
        first_normed[seq] = normed
        first_inverse[seq] = inverse
        first_full[seq, group.own] = (normed * first_gain + first_shift).astype(BF)
        gathers[1].start(seq)

    each(first_norm)

    def feed(seq):
        def step(turn):
            gathers[1].wait(seq, turn)
            share = group.share(turn)
            start = pl.multiple_of(share * rows, 16)
            inner = dot(first_full[seq, share], up_weight[...]) + up_bias
            hidden[seq, pl.ds(start, rows)] = inner
            active = (0.5 * inner * (1.0 + lax.erf(inner * ROOT_HALF))).astype(BF)
            activated[seq, pl.ds(start, rows)] = active
            scatters[1].put(seq, turn, dot(active, down_weight[...]))

        turns(step)

    each(feed)

    def second_norm(seq):
        mixed = scatters[1].take(seq)
        first = first_normed[seq] * first_gain + first_shift
        normed, inverse = norm(first + mixed + down_bias)
        layer_output[seq] = (normed * second_gain + second_shift)[:share_rows].astype(BF)
        place = lax.broadcasted_iota(jnp.int32, (rows, width), 0)
        live = (place < share_rows) & (place + group.own * share_rows < lengths[seq])
        grad = jnp.where(live, pad_rows(cotangent[seq], rows), 0.0)
        back = norm_back(grad, normed, inverse, second_gain)
        sums[0:1] += sum_rows(grad * normed)
        sums[1:2] += sum_rows(grad)
        sums[2:3] += sum_rows(back)
        grad_second[seq] = back
        grad_mixed[seq, group.own] = back.astype(BF)
        gathers[2].start(seq)

    each(second_norm)

    def feed_back(seq):
        def step(turn):
            gathers[2].wait(seq, turn)
            share = group.share(turn)
            start = pl.multiple_of(share * rows, 16)
            grad_active = dot_nt(grad_mixed[seq, share], down_weight[...])
            inner = hidden[seq, pl.ds(start, rows)]
            slope = (
                0.5 * (1.0 + lax.erf(inner * ROOT_HALF))
                + inner * jnp.exp(-0.5 * inner * inner) * INVERSE_ROOT_TAU
            )
            grad = (grad_active * slope).astype(BF)
            grad_hidden[seq, pl.ds(start, rows)] = grad
            sums[6:7] += sum_rows(grad.astype(F32))
            scatters[2].put(seq, turn, dot_nt(grad, up_weight[...]))

        turns(step)

        def weights(step, carry):
            share = step
            start = pl.multiple_of(share * rows, 16)
            down_grad[...] += dot_tn(activated[seq, pl.ds(start, rows)], grad_mixed[seq, share])
            up_grad[...] += dot_tn(first_full[seq, share], grad_hidden[seq, pl.ds(start, rows)])
            return carry

        lax.fori_loop(0, 4, weights, 0)

    each(feed_back)

    def first_back(seq):
        grad = grad_second[seq] + scatters[2].take(seq)
        back = norm_back(grad, first_normed[seq], first_inverse[seq], first_gain)
        sums[3:4] += sum_rows(grad * first_normed[seq])
        sums[4:5] += sum_rows(grad)
        sums[5:6] += sum_rows(back)
        grad_attended[seq] = back

    each(first_back)

    def close(seq):
        for gather in gathers:
            gather.close(seq)

    each(close)


def rear(
    attended_in, full_frames, projected, context, query_weight, key_weight, value_weight, out_weight,
    input_grad, wide_grad, out_grad, sums,
    wide_weight, wide_out, grad_full, grad_context, grad_projected, total,
    outgoing, keep, near, cross, landed,
    gather_send, gather_recv, scatter_send, scatter_recv,
):
    seqs, rows, width = attended_in.shape
    share_rows = input_grad.shape[1]
    heads_width = query_weight.shape[1]
    lanes = wide_weight.shape[1] // 3
    heads = heads_width // HEAD_DIM
    length = 4 * rows
    group = Group()
    gather = Gather(group, grad_full, gather_send, gather_recv)
    scatter = Scatter(group, (outgoing, keep, near, cross, landed), scatter_send, scatter_recv)
    group.greet()

    def each(stage):
        def body(seq, carry):
            stage(seq)
            return carry

        lax.fori_loop(0, seqs, body, 0)

    def turns(step):
        def body(turn, carry):
            step(turn)
            return carry

        lax.fori_loop(0, 4, body, 0)

    def send(seq):
        grad_full[seq, group.own] = attended_in[seq].astype(BF)
        gather.start(seq)

    each(send)
    wide_weight[...] = jnp.zeros_like(wide_weight)
    for index, weight in enumerate((query_weight, key_weight, value_weight)):
        wide_weight[:, index * lanes : index * lanes + heads_width] = weight[...]
    wide_out[...] = jnp.zeros_like(wide_out)
    wide_out[:heads_width] = out_weight[...]
    wide_grad[...] = jnp.zeros_like(wide_grad)
    out_grad[...] = jnp.zeros_like(out_grad)
    sums[...] = jnp.zeros_like(sums)

    def back(seq):
        def step(turn):
            gather.wait(seq, turn)
            share = group.share(turn)
            start = pl.multiple_of(share * rows, 16)
            grad_context[pl.ds(start, rows)] = dot_nt(grad_full[seq, share], wide_out[...]).astype(BF)
            out_grad[...] += dot_tn(context[seq, pl.ds(start, rows)], grad_full[seq, share])

        turns(step)
        total[...] = jnp.zeros_like(total)

        def head_step(head, carry):
            lane = lane_index(length, lanes)
            inside = lane // HEAD_DIM == head
            queries = projected[seq, :, 0:lanes]
            keys = projected[seq, :, lanes : 2 * lanes]
            values = projected[seq, :, 2 * lanes : 3 * lanes]
            picked = jnp.where(inside | (lane == heads_width), queries, jnp.zeros_like(queries))
            scores = dot_nt(keys, picked)
            exponent = jnp.exp(scores - jnp.max(scores, axis=0, keepdims=True))
            weights = exponent * (1.0 / jnp.sum(exponent, axis=0, keepdims=True))
            grads = grad_context[...]
            part = dot(weights.astype(BF), grads)
            total[:, 2 * lanes : 3 * lanes] = jnp.where(inside, part, total[:, 2 * lanes : 3 * lanes])
            slopes = weights * dot_nt(values, jnp.where(inside, grads, jnp.zeros_like(grads)))
            slopes = (slopes - weights * jnp.sum(slopes, axis=0, keepdims=True)).astype(BF)
            part = dot(slopes, queries)
            total[:, lanes : 2 * lanes] = jnp.where(inside, part, total[:, lanes : 2 * lanes])
            part = dot_tn(slopes, keys) * HEAD_DIM ** (-0.5)
            total[:, 0:lanes] = jnp.where(inside, part, total[:, 0:lanes])
            return carry

        lax.fori_loop(0, heads, head_step, 0)

        def finish(turn):
            share = group.share(turn)
            start = pl.multiple_of(share * rows, 16)
            grads = total[pl.ds(start, rows)].astype(BF)
            grad_projected[seq, pl.ds(start, rows)] = grads
            sums[...] += sum_rows(grads.astype(F32))
            scatter.put(seq, turn, dot_nt(grads, wide_weight[...]))

        turns(finish)

        def weights(share, carry):
            start = pl.multiple_of(share * rows, 16)
            wide_grad[...] += dot_tn(full_frames[seq, share], grad_projected[seq, pl.ds(start, rows)])
            return carry

        lax.fori_loop(0, 4, weights, 0)

    each(back)

    def last(seq):
        input_grad[seq] = (scatter.take(seq) + attended_in[seq])[:share_rows]
        gather.close(seq)

    each(last)


def ring_place(index, count):
    return jnp.where(index % 2 == 0, index // 2, count - 1 - index // 2)


def ring_index(place, count):
    return jnp.where(place < count // 2, 2 * place, 2 * (count - 1 - place) + 1)


def grad_ring(count, parts, *refs):
    own = refs[:parts]
    full = refs[parts : 2 * parts]
    first = refs[2 * parts : 3 * parts]
    landed = refs[3 * parts : 4 * parts]
    add_send, add_recv, share_send, share_recv, out_sem = refs[4 * parts : 4 * parts + 5]
    shared = refs[4 * parts + 5 :]
    tensor = lax.axis_index("tensor")
    place = ring_place(lax.axis_index("dp"), count)
    right = ring_index((place + 1) % count, count)
    left = ring_index((place + count - 1) % count, count)
    barrier = pltpu.get_barrier_semaphore()
    for peer in (left, right):
        pl.semaphore_signal(barrier, inc=1, device_id=(peer, tensor), device_id_type=MESH)
    pl.semaphore_wait(barrier, 2)
    steps = count - 1

    def chunk(way, step):
        shift = count - 1 - step if way == 0 else 1 + step
        return (place + shift) % count

    def add_copy(part, way, step):
        source = first[part].at[way] if step == 0 else landed[part].at[way, step - 1]
        return pltpu.make_async_remote_copy(
            src_ref=source,
            dst_ref=landed[part].at[way, step],
            send_sem=add_send.at[part, way, step],
            recv_sem=add_recv.at[part, way, step],
            device_id=(right if way == 0 else left, tensor),
            device_id_type=MESH,
        )

    def share_copy(part, way, step):
        shift = count - step if way == 0 else step
        slot = shared[part].at[(place + shift) % count, way]
        return pltpu.make_async_remote_copy(
            src_ref=slot,
            dst_ref=slot,
            send_sem=share_send.at[part, way, step],
            recv_sem=share_recv.at[part, way, step],
            device_id=(right if way == 0 else left, tensor),
            device_id_type=MESH,
        )

    for part in range(parts):
        for way in range(2):
            first[part][way] = own[part][chunk(way, 0), way].astype(jnp.bfloat16)
            add_copy(part, way, 0).start()
    for step in range(steps):
        for part in range(parts):
            for way in range(2):
                add_copy(part, way, step).wait_recv()
                total = landed[part][way, step].astype(jnp.float32) + own[part][
                    chunk(way, step + 1), way
                ].astype(jnp.float32)
                if step < steps - 1:
                    landed[part][way, step] = total.astype(jnp.bfloat16)
                    add_copy(part, way, step + 1).start()
                else:
                    shared[part][place, way] = total.astype(jnp.bfloat16)
                    share_copy(part, way, 0).start()
    for step in range(steps):
        for part in range(parts):
            for way in range(2):
                share_copy(part, way, step).wait_recv()
                if step < steps - 1:
                    share_copy(part, way, step + 1).start()
    for part in range(parts):
        for way in range(2):
            for step in range(steps):
                add_copy(part, way, step).wait_send()
                share_copy(part, way, step).wait_send()
    outs = [pltpu.make_async_copy(shared[part], full[part], out_sem.at[part]) for part in range(parts)]
    for copy in outs:
        copy.start()
    for copy in outs:
        copy.wait()


def ring_sum(grads, count):
    rows = [grad.shape[0] // (2 * count) for grad in grads]
    blocks = [
        grad.reshape(count, 2, size, grad.shape[1]) for grad, size in zip(grads, rows)
    ]
    parts = len(blocks)
    half = [jax.ShapeDtypeStruct(block.shape, jnp.bfloat16) for block in blocks]
    summed = pl.pallas_call(
        functools.partial(grad_ring, count, parts),
        out_shape=half,
        in_specs=[pl.BlockSpec(memory_space=pltpu.VMEM)] * parts,
        out_specs=[pl.BlockSpec(memory_space=pl.ANY)] * parts,
        scratch_shapes=[pltpu.VMEM(block.shape[1:], jnp.bfloat16) for block in blocks]
        + [
            pltpu.VMEM((2, count - 1) + block.shape[2:], jnp.bfloat16) for block in blocks
        ]
        + [pltpu.SemaphoreType.DMA((parts, 2, count - 1))] * 4
        + [pltpu.SemaphoreType.DMA((parts,))]
        + [pltpu.VMEM(block.shape, jnp.bfloat16) for block in blocks],
        compiler_params=pltpu.CompilerParams(
            collective_id=0, has_side_effects=True, vmem_limit_bytes=60 << 20
        ),
        name="grad_ring",
    )(*blocks)
    return [
        block.reshape(grad.shape).astype(jnp.float32) for block, grad in zip(summed, grads)
    ]


VMEM_SPEC = pl.BlockSpec(memory_space=pltpu.VMEM)


def group_scratch(seqs, rows, width):
    return [
        pltpu.VMEM((seqs, 2, rows, width), BF),
        pltpu.VMEM((seqs, 2, rows, width), F32),
        pltpu.VMEM((seqs, 2, rows, width), BF),
        pltpu.VMEM((seqs, rows, width), BF),
        pltpu.VMEM((seqs, rows, width), BF),
    ]


def shards(
    frames,
    cotangent,
    lengths,
    query_weight,
    query_bias,
    key_weight,
    value_weight,
    value_bias,
    out_weight,
    out_bias,
    first_gain,
    first_shift,
    up_weight,
    up_bias,
    down_weight,
    down_bias,
    second_gain,
    second_shift,
):
    seqs, share_rows, width = frames.shape
    rows = up_to(share_rows, 16)
    length = 4 * rows
    heads_width = query_weight.shape[1]
    inner = up_weight.shape[1]
    lanes = up_to(heads_width + 1, 128)
    pad = lanes - heads_width
    projection_bias = jnp.concatenate(
        [
            query_bias,
            jnp.full((1,), HEAD_DIM**0.5, F32),
            jnp.zeros((pad - 1 + lanes,), F32),
            value_bias,
            jnp.zeros((pad,), F32),
        ]
    )[None]
    vectors = jnp.stack(
        [out_bias, first_gain, first_shift, down_bias, second_gain, second_shift, up_bias]
    )
    shape = jax.ShapeDtypeStruct
    (
        layer_output, full_frames, projected, context, grad_attended, up_grad, down_grad, sums,
    ) = pl.pallas_call(
        front,
        out_shape=[
            shape(frames.shape, BF),
            shape((seqs, 4, rows, width), BF),
            shape((seqs, length, 3 * lanes), BF),
            shape((seqs, length, lanes), BF),
            shape((seqs, rows, width), F32),
            shape(up_weight.shape, F32),
            shape(down_weight.shape, F32),
            shape((8, width), F32),
        ],
        in_specs=[pl.BlockSpec(memory_space=pltpu.SMEM)] + [VMEM_SPEC] * 10,
        out_specs=[VMEM_SPEC] * 8,
        scratch_shapes=[
            pltpu.VMEM((width, 3 * lanes), BF),
            pltpu.VMEM((lanes, width), BF),
            pltpu.VMEM((seqs, rows, width), F32),
            pltpu.VMEM((seqs, rows, 1), F32),
            pltpu.VMEM((seqs, 4, rows, width), BF),
            pltpu.VMEM((seqs, length, inner), F32),
            pltpu.VMEM((seqs, length, inner), BF),
            pltpu.VMEM((seqs, rows, width), F32),
            pltpu.VMEM((seqs, 4, rows, width), BF),
            pltpu.VMEM((seqs, length, inner), BF),
        ]
        + group_scratch(seqs, rows, width)
        + [pltpu.SemaphoreType.DMA((3, seqs, 3))] * 4,
        compiler_params=pltpu.CompilerParams(
            collective_id=1, has_side_effects=True, vmem_limit_bytes=VMEM_BYTES
        ),
        name="front",
    )(
        lengths, frames, cotangent, query_weight, key_weight, value_weight, projection_bias,
        out_weight, up_weight, down_weight, vectors,
    )
    input_grad, wide_grad, out_grad, rear_sums = pl.pallas_call(
        rear,
        out_shape=[
            shape(frames.shape, F32),
            shape((width, 3 * lanes), F32),
            shape((lanes, width), F32),
            shape((1, 3 * lanes), F32),
        ],
        in_specs=[VMEM_SPEC] * 8,
        out_specs=[VMEM_SPEC] * 4,
        scratch_shapes=[
            pltpu.VMEM((width, 3 * lanes), BF),
            pltpu.VMEM((lanes, width), BF),
            pltpu.VMEM((seqs, 4, rows, width), BF),
            pltpu.VMEM((length, lanes), BF),
            pltpu.VMEM((seqs, length, 3 * lanes), BF),
            pltpu.VMEM((length, 3 * lanes), F32),
        ]
        + group_scratch(seqs, rows, width)
        + [pltpu.SemaphoreType.DMA((seqs, 3))] * 4,
        compiler_params=pltpu.CompilerParams(
            collective_id=2, has_side_effects=True, vmem_limit_bytes=VMEM_BYTES
        ),
        name="rear",
    )(
        grad_attended, full_frames, projected, context, query_weight, key_weight, value_weight, out_weight,
    )
    count = lax.axis_size("dp")
    large = [wide_grad, out_grad, up_grad, down_grad]
    if count % 2 == 0 and all(grad.shape[0] % (16 * count) == 0 for grad in large):
        large = ring_sum(large, count)
    else:
        large = lax.psum(large, "dp")
    wide_grad, out_grad, up_grad, down_grad = large
    rear_sums, up_bias_grad = lax.psum((rear_sums[0], sums[6]), "dp")
    small = lax.psum(sums[:6], ("dp", "tensor"))
    return (
        layer_output,
        input_grad,
        wide_grad[:, :heads_width],
        rear_sums[:heads_width],
        wide_grad[:, lanes : lanes + heads_width],
        wide_grad[:, 2 * lanes : 2 * lanes + heads_width],
        rear_sums[2 * lanes : 2 * lanes + heads_width],
        out_grad[:heads_width],
        small[5],
        small[3],
        small[4],
        up_grad,
        up_bias_grad,
        down_grad,
        small[2],
        small[0],
        small[1],
    )


def solution(mesh):
    return jax.shard_map(
        shards,
        mesh=mesh,
        in_specs=(
            P("dp", "tensor", None),
            P("dp", "tensor", None),
            P("dp"),
            P(None, "tensor"),
            P("tensor"),
            P(None, "tensor"),
            P(None, "tensor"),
            P("tensor"),
            P("tensor", None),
            P(),
            P(),
            P(),
            P(None, "tensor"),
            P("tensor"),
            P("tensor", None),
            P(),
            P(),
            P(),
        ),
        out_specs=(
            P("dp", "tensor", None),
            P("dp", "tensor", None),
            P(None, "tensor"),
            P("tensor"),
            P(None, "tensor"),
            P(None, "tensor"),
            P("tensor"),
            P("tensor", None),
            P(),
            P(),
            P(),
            P(None, "tensor"),
            P("tensor"),
            P("tensor", None),
            P(),
            P(),
            P(),
        ),
        check_vma=False,
    )
```

time: 609 us -> 327 us (0.54)
  waiting for transfers between devices: 231 us -> 0 us
  Pallas kernels: 86.1 us -> 243 us
  matrix products: 127 us -> 0 us
  other arithmetic: 55 us -> 5.4 us
  between operations: 15.2 us -> 0.75 us
  local copies, waits for them, and re-layouts: 25.7 us -> 19 us
    pallas_call x0 -> x2, Pallas kernels: none -> 159 us  [the longest x1 103 us: shards(): pl.pallas_call(front, out_shape=[shape(frames.shape, BF), shape((seqs, 4,...]
    reduce_scatter x8 -> x0, waiting for transfers between devices: 145 us -> none  [the longest x2 51 us: ffn_backward(): lax.psum_scatter(jnp.einsum('rf,df->rd', grad_hidden, up_weight, preferre...]
    dot_general x48 -> x0, matrix products: 127 us -> none  [the longest x2 17.4 us: layer_forward(): jnp.dot(first_full, up_weight, preferred_element_type=jnp.float32) + up_bias]
    all_gather x8 -> x0, waiting for transfers between devices: 85 us -> none  [the longest x2 33 us: layer_forward(): lax.all_gather(first.astype(jnp.bfloat16), 'tensor', axis=0, tiled=True)]
    convert_element_type x7 -> x0, other arithmetic: 25.8 us -> none  [the longest x2 19 us: attention_backward(): grad_scores = (attention * (grad_attention - jnp.sum(attention * grad_att...]
    reduce_sum x12 -> x0, other arithmetic: 15 us -> none  [the longest x2 3.21 us: norm_back(): jnp.sum(grad_out * normed, axis=0)]
    unnamed x145 -> x20, local copies, waits for them, and re-layouts: 14.6 us -> 10.7 us
  transfers between devices with their start and end apart: 16 -> 0, of which waited for: 12 -> 0; matrix products, arithmetic and copies ran while one was open for 23% -> 0% of each run, Pallas kernels for 14% -> 0%
where the time goes in v2:
time: 327 us; the launch traced here: 326 us
  Pallas kernels  243 us (74%)
  blocking collectives  57.6 us (18%)
  local copies, waits for them, and re-layouts  19 us (6%)
  other arithmetic  5.4 us (2%)
    pallas_call x1, Pallas kernels, shards(): pl.pallas_call(front, out_shape=[shape(frames.shape, BF), shape((seqs, 4,...  103 us
    pallas_call x1, Pallas kernels, ring_sum(): pl.pallas_call(functools.partial(grad_ring, count, parts), out_shape=half...  84.7 us
    pallas_call x1, Pallas kernels, shards(): pl.pallas_call(rear, out_shape=[shape(frames.shape, F32), shape((width, 3...  56 us
    psum x1, blocking collectives, shards(): small = lax.psum(sums[:6], ('dp', 'tensor'))  37 us
    psum x1, blocking collectives, shards(): rear_sums, up_bias_grad = lax.psum((rear_sums[0], sums[6]), 'dp')  20.6 us
    unnamed x20, local copies, waits for them, and re-layouts  10.7 us

profile of v2, /device:TPU:0, one launch (start us, length us, event | category | flops | bytes accessed | tf_op | source)
XLA Modules:
  0.0 326.1 jit_solution(14069392281983075812)
XLA Ops:
  0.7 1.9 copy.35.query_weight
  2.5 1.9 copy.36.key_weight
  4.4 1.9 copy.37.value_weight
  6.3 0.7 stack.24
  7.0 0.7 stack.25
  7.7 0.7 stack.26
  8.4 0.7 stack.27
  9.1 0.7 stack.28
  9.7 0.7 stack.29
  10.4 0.7 stack.30
  11.1 0.6 stack.31.vectors
  11.8 0.8 concatenate.3
  12.5 0.6 broadcast_in_dim.11.projection_bias
  13.1 102.6 %front.1 = (bf16[2,200,768]{2,1,0:T(8,128)(2,1)}, bf16[2,4,208,768]{3,2,1,0:T(8,128)(2,1)}, bf16[2,832,768]{2,1,0:T(8,128)(2,1)}, bf16[2,832,256]{2,1,0:T(8,128)...) custom-call(s32[2]{0:T(128)} %lengths.1, ...), custom_call_target="tpu_custom_call" | custom-call | tf_op jit(solution)/shard_map/front/pallas_call | solution.py:654
  115.7 56.0 %rear.1 = (f32[2,200,768]{2,1,0:T(8,128)}, f32[768,768]{1,0:T(8,128)}, f32[256,768]{1,0:T(8,128)}, f32[1,768]{1,0:T(1,128)}) custom-call(f32[2,208,768]{2,1,0:T(8,128)} %get-tuple-element.34.attended_in, bf16[2,4,208,768]{3,2,1,0:T(8,128)(2,1)} %get-tuple-element.35.full_frames, bf16[2,832,768]{2,1,0:T(8,128)(2,1)} %get-tuple-element.36.projected, ...), custom_call_target="tpu_custom_call" | custom-call | tf_op jit(solution)/shard_map/rear/pallas_call | solution.py:690
  171.8 84.7 %grad_ring.1 = (bf16[8,2,48,768]{3,2,1,0:T(8,128)(2,1)}, bf16[8,2,16,768]{3,2,1,0:T(8,128)(2,1)}, bf16[8,2,48,768]{3,2,1,0:T(8,128)(2,1)}, bf16[8,2,48,768]{3,2,1,0:T(8,128)(2,1)}) custom-call(f32[8,2,48,768]{3,2,1,0:T(8,128)} %bitcast.19, f32[8,2,16,768]{3,2,1,0:T(8,128)} %bitcast.20, f32[8,2,48,768]{3,2,1,0:T(8,128)} %bitcast.17, f32[8,2,48,768]{3,2,1,0:T(8,128)} %bitcast.18), custom_call_target="tpu_custom_call" | custom-call | tf_op jit(solution)/shard_map/grad_ring/pallas_call | solution.py:577
  256.5 0.0 copy-start.1
  256.5 4.3 %bitcast_convert_fusion = (f32[768,768]{1,0:T(8,128)}, f32[768,768]{1,0:T(8,128)}) fusion(bf16[8,2,48,768]{3,2,1,0:T(8,128)(2,1)} %get-tuple-element.48, bf16[8,2,48,768]{3,2,1,0:T(8,128)(2,1)} %get-tuple-element.47), kind=kLoop, calls=%fused_computation | loop fusion | flops 1179648 | bytes 7077888 | tf_op jit(solution)/shard_map/convert_element_type | solution.py:595
  260.8 0.0 copy-done.1
  260.8 0.2 bitcast_convert_fusion.2
  261.0 0.2 fusion
  261.2 0.0 copy-start.3
  261.2 1.1 copy.44
  262.3 0.0 copy-start.5
  262.3 0.0 copy-start.4
  262.3 0.0 copy-start.2
  262.3 1.1 copy.45
  263.4 0.0 copy-start
  263.4 1.1 copy.46
  264.4 0.0 copy-done.3
  264.5 0.9 bitcast_convert_fusion.3
  265.3 0.0 copy-done.5
  265.4 0.0 copy-done.4
  265.4 20.6 %all-reduce = (f32[768]{0:T(1024)S(1)}, f32[768]{0:T(1024)}) all-reduce(f32[768]{0:T(1024)S(1)} %reduce, f32[768]{0:T(1024)S(1)} %slice_reduce_fusion.6), channel_id=1, replica_groups=mesh['dp'=8,'tensor'=4] {'dp'}, use_global_device_ids=true, to_apply=%region_0.0 | all-reduce | flops 1536 | bytes 12288 | tf_op jit(solution)/shard_map/psum | solution.py:724
  286.0 0.6 fusion.1
  286.5 37.0 %psum.22 = f32[6,768]{1,0:T(8,128)S(1)} all-reduce(f32[6,768]{1,0:T(8,128)S(1)} %bitcast.21), channel_id=1, replica_groups=mesh['dp'=8,'tensor'=4] {'dp','tensor'}, use_global_device_ids=true, to_apply=%region_1.0 | all-reduce | flops 4608 | bytes 36864 | tf_op jit(solution)/shard_map/psum | solution.py:725
  323.6 0.6 slice_reduce_fusion
  324.2 0.0 copy-done.2
  324.2 0.8 copy.49
  325.0 0.0 copy-done
  325.0 1.0 copy.50
  (5 shorter events, 0.1 us)
Async XLA Ops:
  256.5 4.3 %copy-start.1 = (bf16[8,2,48,768]{3,2,1,0:T(8,128)(2,1)S(1)}, bf16[8,2,48,768]{3,2,1,0:T(8,128)(2,1)}, u32[]{:S(2)}) copy-start(bf16[8,2,48,768]{3,2,1,0:T(8,128)(2,1)} %get-tuple-element.43) | copy-start | bytes 3538948
  261.2 3.2 copy-start.3
  262.3 3.0 copy-start.5
  262.3 3.1 copy-start.4
  262.3 61.9 %copy-start.2 = (bf16[2,200,768]{2,1,0:T(8,128)(2,1)S(1)}, bf16[2,200,768]{2,1,0:T(8,128)(2,1)}, u32[]{:S(2)}) copy-start(bf16[2,200,768]{2,1,0:T(8,128)(2,1)} %get-tuple-element.81) | copy-start | bytes 1843204
  263.4 61.7 %copy-start = (f32[2,200,768]{2,1,0:T(8,128)S(1)}, f32[2,200,768]{2,1,0:T(8,128)}, u32[]{:S(2)}) copy-start(f32[2,200,768]{2,1,0:T(8,128)} %get-tuple-element.82) | copy-start | bytes 3686404

commit v3 on v2

--- a/solution.py
+++ b/solution.py
@@ -50,11 +50,12 @@
         self.mate = self.y * 2 + (1 - self.core)
         self.far = (1 - self.y) * 2 + self.core
 
-    def greet(self):
+    def greet(self, dp_peers=()):
         barrier = pltpu.get_barrier_semaphore()
-        for peer in (self.mate, self.far):
-            pl.semaphore_signal(barrier, inc=1, device_id=(self.dp, peer), device_id_type=MESH)
-        pl.semaphore_wait(barrier, 2)
+        peers = [(self.dp, self.mate), (self.dp, self.far)] + [(peer, self.own) for peer in dp_peers]
+        for peer in peers:
+            pl.semaphore_signal(barrier, inc=1, device_id=peer, device_id_type=MESH)
+        pl.semaphore_wait(barrier, len(peers))
 
     def share(self, turn):
         late = turn // 2
@@ -186,23 +187,28 @@
 
 
 def front(
-    lengths, frames, cotangent, query_weight, key_weight, value_weight, projection_bias,
-    out_weight, up_weight, down_weight, vectors,
+    lengths, frames, cotangent, query_weight, key_weight, value_weight, query_bias, value_bias,
+    out_weight, out_bias_row, first_gain_row, first_shift_row, up_weight, up_bias_row,
+    down_weight, down_bias_row, second_gain_row, second_shift_row,
     layer_output, full_frames, projected, context, grad_attended, up_grad, down_grad, sums,
-    wide_weight, wide_out, first_normed, first_inverse, first_full, hidden, activated,
+    wide_weight, wide_out, projection_bias, first_normed, first_inverse, first_full, hidden, activated,
     grad_second, grad_mixed, grad_hidden,
     outgoing, keep, near, cross, landed,
     gather_send, gather_recv, scatter_send, scatter_recv,
 ):
     seqs, share_rows, width = frames.shape
     rows = full_frames.shape[2]
-    heads_width = query_weight.shape[1]
-    lanes = wide_weight.shape[1] // 3
+    heads_width = query_weight.shape[0]
+    lanes = wide_weight.shape[0] // 3
     heads = heads_width // HEAD_DIM
     length = 4 * rows
     group = Group()
     out_bias, first_gain, first_shift, down_bias, second_gain, second_shift, up_bias = (
-        vectors[index : index + 1] for index in range(7)
+        row[...].reshape(1, row.shape[0])
+        for row in (
+            out_bias_row, first_gain_row, first_shift_row, down_bias_row, second_gain_row,
+            second_shift_row, up_bias_row,
+        )
     )
     buffers = (outgoing, keep, near, cross, landed)
     gathers = [
@@ -236,9 +242,14 @@
     each(send_frames)
     wide_weight[...] = jnp.zeros_like(wide_weight)
     for index, weight in enumerate((query_weight, key_weight, value_weight)):
-        wide_weight[:, index * lanes : index * lanes + heads_width] = weight[...]
+        wide_weight[index * lanes : index * lanes + heads_width] = weight[...]
     wide_out[...] = jnp.zeros_like(wide_out)
     wide_out[:heads_width] = out_weight[...]
+    projection_bias[...] = jnp.where(
+        lane_index(1, 3 * lanes) == heads_width, HEAD_DIM**0.5, 0.0
+    )
+    projection_bias[:, :heads_width] = query_bias[...].reshape(1, heads_width)
+    projection_bias[:, 2 * lanes : 2 * lanes + heads_width] = value_bias[...].reshape(1, heads_width)
     sums[...] = jnp.zeros_like(sums)
     up_grad[...] = jnp.zeros_like(up_grad)
     down_grad[...] = jnp.zeros_like(down_grad)
@@ -248,7 +259,7 @@
             turn = (1 - step // 2) * (3 - step) + (step // 2) * (step - 2)
             gathers[0].wait(seq, turn)
             share = group.share(turn)
-            result = dot(full_frames[seq, share], wide_weight[...]) + projection_bias[...]
+            result = dot_nt(full_frames[seq, share], wide_weight[...]) + projection_bias[...]
             place = lax.broadcasted_iota(jnp.int32, (rows, lanes), 0)
             dead = (place >= share_rows) | (place + share * share_rows >= lengths[seq])
             flag = jnp.where(dead & (lane_index(rows, lanes) == heads_width), MASKED, 0.0)
@@ -374,30 +385,179 @@
     each(close)
 
 
+class Ring:
+    def __init__(self, group, count, own, opening, landed, shared, sems):
+        self.group, self.count, self.steps = group, count, count - 1
+        self.own, self.opening, self.landed, self.shared = own, opening, landed, shared
+        self.add_send, self.add_recv, self.share_send, self.share_recv = sems
+        self.rows = own.shape[0] // (2 * count)
+        self.place, self.right, self.left = ring_peers(group.dp, count)
+
+    def _own(self, way, step):
+        shift = self.count - 1 - step if way == 0 else 1 + step
+        chunk = (self.place + shift) % self.count
+        start = pl.multiple_of((2 * chunk + way) * self.rows, 16)
+        return self.own[pl.ds(start, self.rows)]
+
+    def _copy(self, source, target, send, recv, way):
+        return pltpu.make_async_remote_copy(
+            src_ref=source,
+            dst_ref=target,
+            send_sem=send,
+            recv_sem=recv,
+            device_id=(self.right if way == 0 else self.left, self.group.own),
+            device_id_type=MESH,
+        )
+
+    def _add(self, way, step, source=None):
+        target = self.landed.at[way, step]
+        return self._copy(
+            target if source is None else source,
+            target,
+            self.add_send.at[way, step],
+            self.add_recv.at[way, step],
+            way,
+        )
+
+    def _share(self, way, step):
+        shift = self.count - step if way == 0 else step
+        slot = self.shared.at[(self.place + shift) % self.count, way]
+        return self._copy(
+            slot, slot, self.share_send.at[way, step], self.share_recv.at[way, step], way
+        )
+
+    def open(self):
+        for way in range(2):
+            self.opening[way] = self._own(way, 0).astype(BF)
+            self._add(way, 0, self.opening.at[way]).start()
+
+    def advance(self, step):
+        last = self.steps - 1
+        for way in range(2):
+            if step < self.steps:
+                self._add(way, step).wait_recv()
+                total = self.landed[way, step].astype(F32) + self._own(way, step + 1)
+                if step < last:
+                    self.landed[way, step] = total.astype(BF)
+                    self._add(way, step + 1, self.landed.at[way, step]).start()
+                else:
+                    self.shared[self.place, way] = total.astype(BF)
+                    self._share(way, 0).start()
+            else:
+                turn = step - self.steps
+                self._share(way, turn).wait_recv()
+                if turn < last:
+                    self._share(way, turn + 1).start()
+
+    def close(self):
+        for way in range(2):
+            for step in range(self.steps):
+                self._add(way, step).wait_send()
+                self._share(way, step).wait_send()
+
+
+def ring_peers(index, count):
+    odd = index % 2
+    place = (1 - odd) * (index // 2) + odd * (count - 1 - index // 2)
+
+    def at(spot):
+        late = spot // (count // 2)
+        return (1 - late) * 2 * spot + late * (2 * (count - 1 - spot) + 1)
+
+    return place, at((place + 1) % count), at((place + count - 1) % count)
+
+
+def halving_peers(index, count):
+    peers = []
+    bit = 1
+    while bit < count:
+        peers.append(index + bit * (1 - 2 * ((index // bit) % 2)))
+        bit *= 2
+    return peers
+
+
+class Totals:
+    def __init__(self, group, peers, outgoing, arriving, send, recv, shared):
+        self.group, self.shared = group, shared
+        self.outgoing, self.arriving, self.send, self.recv = outgoing, arriving, send, recv
+        own = group.own
+        self.peers = [(group.dp, group.mate), (group.dp, group.far)] + [(peer, own) for peer in peers]
+
+    def _copy(self, level):
+        return pltpu.make_async_remote_copy(
+            src_ref=self.outgoing.at[level],
+            dst_ref=self.arriving.at[level],
+            send_sem=self.send.at[level],
+            recv_sem=self.recv.at[level],
+            device_id=self.peers[level],
+            device_id_type=MESH,
+        )
+
+    def begin(self, level, rows):
+        self.outgoing[level] = rows
+        self._copy(level).start()
+
+    def end(self, level):
+        self._copy(level).wait()
+        other = self.arriving[level]
+        if level < 2:
+            place = lax.broadcasted_iota(jnp.int32, other.shape, 0)
+            other = jnp.where(place < self.shared, other, 0.0)
+        return self.outgoing[level] + other
+
+
 def rear(
+    count,
     attended_in, full_frames, projected, context, query_weight, key_weight, value_weight, out_weight,
-    input_grad, wide_grad, out_grad, sums,
-    wide_weight, wide_out, grad_full, grad_context, grad_projected, total,
-    outgoing, keep, near, cross, landed,
-    gather_send, gather_recv, scatter_send, scatter_recv,
+    up_grad, down_grad, front_sums,
+    input_grad, *refs,
 ):
+    outs, refs = refs[: 4 if count else 2], refs[4 if count else 2 :]
+    (
+        wide_weight, wide_out, grad_full, grad_context, grad_projected, total,
+        outgoing, keep, near, cross, landed,
+        gather_send, gather_recv, scatter_send, scatter_recv,
+    ), refs = refs[:15], refs[15:]
     seqs, rows, width = attended_in.shape
     share_rows = input_grad.shape[1]
-    heads_width = query_weight.shape[1]
-    lanes = wide_weight.shape[1] // 3
+    heads_width = query_weight.shape[0]
+    lanes = wide_weight.shape[0] // 3
     heads = heads_width // HEAD_DIM
     length = 4 * rows
     group = Group()
     gather = Gather(group, grad_full, gather_send, gather_recv)
     scatter = Scatter(group, (outgoing, keep, near, cross, landed), scatter_send, scatter_recv)
-    group.greet()
-
-    def each(stage):
-        def body(seq, carry):
-            stage(seq)
-            return carry
-
-        lax.fori_loop(0, seqs, body, 0)
+    if count:
+        sums = outs[3]
+        heads_grad, opening, ring_landed, ring_shared = refs[:4]
+        add_send, add_recv, share_send, share_recv, out_sem = refs[4:9]
+        small_out, small_in, small_send, small_recv = refs[9:13]
+        _, right, left = ring_peers(group.dp, count)
+        pairs = halving_peers(group.dp, count)
+        group.greet([right, left] + pairs)
+        rings = [
+            Ring(
+                group,
+                count,
+                own,
+                opening.at[index],
+                ring_landed.at[index],
+                ring_shared.at[index],
+                [sem.at[index] for sem in (add_send, add_recv, share_send, share_recv)],
+            )
+            for index, own in enumerate((up_grad, down_grad, heads_grad))
+        ]
+        totals = Totals(group, pairs, small_out, small_in, small_send, small_recv, 6)
+    else:
+        heads_grad, sums = outs
+        group.greet()
+    ahead = [0]
+
+    def poll():
+        if count and ahead[0] < 2 * (count - 1):
+            for ring in rings[:2]:
+                ring.advance(ahead[0])
+            ahead[0] += 1
 
     def turns(step):
         def body(turn, carry):
@@ -406,32 +566,37 @@
 
         lax.fori_loop(0, 4, body, 0)
 
-    def send(seq):
+    for seq in range(seqs):
         grad_full[seq, group.own] = attended_in[seq].astype(BF)
         gather.start(seq)
-
-    each(send)
+    if count:
+        for ring in rings[:2]:
+            ring.open()
+        totals.begin(0, front_sums[...])
     wide_weight[...] = jnp.zeros_like(wide_weight)
     for index, weight in enumerate((query_weight, key_weight, value_weight)):
-        wide_weight[:, index * lanes : index * lanes + heads_width] = weight[...]
+        wide_weight[index * lanes : index * lanes + heads_width] = weight[...]
     wide_out[...] = jnp.zeros_like(wide_out)
     wide_out[:heads_width] = out_weight[...]
-    wide_grad[...] = jnp.zeros_like(wide_grad)
-    out_grad[...] = jnp.zeros_like(out_grad)
+    heads_grad[...] = jnp.zeros_like(heads_grad)
     sums[...] = jnp.zeros_like(sums)
 
-    def back(seq):
+    for seq in range(seqs):
+
         def step(turn):
             gather.wait(seq, turn)
             share = group.share(turn)
             start = pl.multiple_of(share * rows, 16)
             grad_context[pl.ds(start, rows)] = dot_nt(grad_full[seq, share], wide_out[...]).astype(BF)
-            out_grad[...] += dot_tn(context[seq, pl.ds(start, rows)], grad_full[seq, share])
+            heads_grad[3 * heads_width :] += dot_tn(
+                context[seq, pl.ds(start, rows)], grad_full[seq, share]
+            )[:heads_width]
 
         turns(step)
+        poll()
         total[...] = jnp.zeros_like(total)
 
-        def head_step(head, carry):
+        def head_step(head):
             lane = lane_index(length, lanes)
             inside = lane // HEAD_DIM == head
             queries = projected[seq, :, 0:lanes]
@@ -450,153 +615,77 @@
             total[:, lanes : 2 * lanes] = jnp.where(inside, part, total[:, lanes : 2 * lanes])
             part = dot_tn(slopes, keys) * HEAD_DIM ** (-0.5)
             total[:, 0:lanes] = jnp.where(inside, part, total[:, 0:lanes])
-            return carry
-
-        lax.fori_loop(0, heads, head_step, 0)
+
+        for head in range(heads):
+            head_step(head)
+            poll()
 
         def finish(turn):
             share = group.share(turn)
             start = pl.multiple_of(share * rows, 16)
             grads = total[pl.ds(start, rows)].astype(BF)
-            grad_projected[seq, pl.ds(start, rows)] = grads
-            sums[...] += sum_rows(grads.astype(F32))
-            scatter.put(seq, turn, dot_nt(grads, wide_weight[...]))
+            grad_projected[pl.ds(start, rows)] = grads
+            sums[7:8] += sum_rows(grads.astype(F32))
+            scatter.put(seq, turn, dot(grads, wide_weight[...]))
 
         turns(finish)
+        poll()
 
         def weights(share, carry):
             start = pl.multiple_of(share * rows, 16)
-            wide_grad[...] += dot_tn(full_frames[seq, share], grad_projected[seq, pl.ds(start, rows)])
+            for index in range(3):
+                heads_grad[index * heads_width : (index + 1) * heads_width] += dot_tn(
+                    grad_projected[pl.ds(start, rows), index * lanes : (index + 1) * lanes],
+                    full_frames[seq, share],
+                )[:heads_width]
             return carry
 
         lax.fori_loop(0, 4, weights, 0)
-
-    each(back)
-
-    def last(seq):
+        poll()
+        if count and seq == 0:
+            totals.begin(1, totals.end(0))
+
+    if count:
+        rings[2].open()
+        place = lax.broadcasted_iota(jnp.int32, front_sums.shape, 0)
+        rows_sum = totals.end(1)
+        totals.begin(2, jnp.where(place == 7, sums[...], rows_sum))
+    else:
+        sums[:7] = front_sums[:7]
+
+    for seq in range(seqs):
         input_grad[seq] = (scatter.take(seq) + attended_in[seq])[:share_rows]
         gather.close(seq)
 
-    each(last)
-
-
-def ring_place(index, count):
-    return jnp.where(index % 2 == 0, index // 2, count - 1 - index // 2)
-
-
-def ring_index(place, count):
-    return jnp.where(place < count // 2, 2 * place, 2 * (count - 1 - place) + 1)
-
-
-def grad_ring(count, parts, *refs):
-    own = refs[:parts]
-    full = refs[parts : 2 * parts]
-    first = refs[2 * parts : 3 * parts]
-    landed = refs[3 * parts : 4 * parts]
-    add_send, add_recv, share_send, share_recv, out_sem = refs[4 * parts : 4 * parts + 5]
-    shared = refs[4 * parts + 5 :]
-    tensor = lax.axis_index("tensor")
-    place = ring_place(lax.axis_index("dp"), count)
-    right = ring_index((place + 1) % count, count)
-    left = ring_index((place + count - 1) % count, count)
-    barrier = pltpu.get_barrier_semaphore()
-    for peer in (left, right):
-        pl.semaphore_signal(barrier, inc=1, device_id=(peer, tensor), device_id_type=MESH)
-    pl.semaphore_wait(barrier, 2)
-    steps = count - 1
-
-    def chunk(way, step):
-        shift = count - 1 - step if way == 0 else 1 + step
-        return (place + shift) % count
-
-    def add_copy(part, way, step):
-        source = first[part].at[way] if step == 0 else landed[part].at[way, step - 1]
-        return pltpu.make_async_remote_copy(
-            src_ref=source,
-            dst_ref=landed[part].at[way, step],
-            send_sem=add_send.at[part, way, step],
-            recv_sem=add_recv.at[part, way, step],
-            device_id=(right if way == 0 else left, tensor),
-            device_id_type=MESH,
-        )
-
-    def share_copy(part, way, step):
-        shift = count - step if way == 0 else step
-        slot = shared[part].at[(place + shift) % count, way]
-        return pltpu.make_async_remote_copy(
-            src_ref=slot,
-            dst_ref=slot,
-            send_sem=share_send.at[part, way, step],
-            recv_sem=share_recv.at[part, way, step],
-            device_id=(right if way == 0 else left, tensor),
-            device_id_type=MESH,
-        )
-
-    for part in range(parts):
-        for way in range(2):
-            first[part][way] = own[part][chunk(way, 0), way].astype(jnp.bfloat16)
-            add_copy(part, way, 0).start()
-    for step in range(steps):
-        for part in range(parts):
-            for way in range(2):
-                add_copy(part, way, step).wait_recv()
-                total = landed[part][way, step].astype(jnp.float32) + own[part][
-                    chunk(way, step + 1), way
-                ].astype(jnp.float32)
-                if step < steps - 1:
-                    landed[part][way, step] = total.astype(jnp.bfloat16)
-                    add_copy(part, way, step + 1).start()
+    if count:
+        level = 2
+        last = len(pairs) + 1
+        for step in range(2 * (count - 1)):
+            poll()
+            rings[2].advance(step)
+            if step % 3 == 2 and level <= last:
+                rows_sum = totals.end(level)
+                level += 1
+                if level <= last:
+                    totals.begin(level, rows_sum)
                 else:
-                    shared[part][place, way] = total.astype(jnp.bfloat16)
-                    share_copy(part, way, 0).start()
-    for step in range(steps):
-        for part in range(parts):
-            for way in range(2):
-                share_copy(part, way, step).wait_recv()
-                if step < steps - 1:
-                    share_copy(part, way, step + 1).start()
-    for part in range(parts):
-        for way in range(2):
-            for step in range(steps):
-                add_copy(part, way, step).wait_send()
-                share_copy(part, way, step).wait_send()
-    outs = [pltpu.make_async_copy(shared[part], full[part], out_sem.at[part]) for part in range(parts)]
-    for copy in outs:
-        copy.start()
-    for copy in outs:
-        copy.wait()
-
-
-def ring_sum(grads, count):
-    rows = [grad.shape[0] // (2 * count) for grad in grads]
-    blocks = [
-        grad.reshape(count, 2, size, grad.shape[1]) for grad, size in zip(grads, rows)
-    ]
-    parts = len(blocks)
-    half = [jax.ShapeDtypeStruct(block.shape, jnp.bfloat16) for block in blocks]
-    summed = pl.pallas_call(
-        functools.partial(grad_ring, count, parts),
-        out_shape=half,
-        in_specs=[pl.BlockSpec(memory_space=pltpu.VMEM)] * parts,
-        out_specs=[pl.BlockSpec(memory_space=pl.ANY)] * parts,
-        scratch_shapes=[pltpu.VMEM(block.shape[1:], jnp.bfloat16) for block in blocks]
-        + [
-            pltpu.VMEM((2, count - 1) + block.shape[2:], jnp.bfloat16) for block in blocks
+                    sums[...] = rows_sum
+        while ahead[0] < 2 * (count - 1):
+            poll()
+        copies = [
+            pltpu.make_async_copy(ring_shared.at[index], outs[index], out_sem.at[index])
+            for index in range(3)
         ]
-        + [pltpu.SemaphoreType.DMA((parts, 2, count - 1))] * 4
-        + [pltpu.SemaphoreType.DMA((parts,))]
-        + [pltpu.VMEM(block.shape, jnp.bfloat16) for block in blocks],
-        compiler_params=pltpu.CompilerParams(
-            collective_id=0, has_side_effects=True, vmem_limit_bytes=60 << 20
-        ),
-        name="grad_ring",
-    )(*blocks)
-    return [
-        block.reshape(grad.shape).astype(jnp.float32) for block, grad in zip(summed, grads)
-    ]
+        for copy in copies:
+            copy.start()
+        for ring in rings:
+            ring.close()
+        for copy in copies:
+            copy.wait()
 
 
 VMEM_SPEC = pl.BlockSpec(memory_space=pltpu.VMEM)
+ANY_SPEC = pl.BlockSpec(memory_space=pl.ANY)
 
 
 def group_scratch(seqs, rows, width):
@@ -635,19 +724,7 @@
     heads_width = query_weight.shape[1]
     inner = up_weight.shape[1]
     lanes = up_to(heads_width + 1, 128)
-    pad = lanes - heads_width
-    projection_bias = jnp.concatenate(
-        [
-            query_bias,
-            jnp.full((1,), HEAD_DIM**0.5, F32),
-            jnp.zeros((pad - 1 + lanes,), F32),
-            value_bias,
-            jnp.zeros((pad,), F32),
-        ]
-    )[None]
-    vectors = jnp.stack(
-        [out_bias, first_gain, first_shift, down_bias, second_gain, second_shift, up_bias]
-    )
+    query_rows, key_rows, value_rows = query_weight.T, key_weight.T, value_weight.T
     shape = jax.ShapeDtypeStruct
     (
         layer_output, full_frames, projected, context, grad_attended, up_grad, down_grad, sums,
@@ -663,11 +740,12 @@
             shape(down_weight.shape, F32),
             shape((8, width), F32),
         ],
-        in_specs=[pl.BlockSpec(memory_space=pltpu.SMEM)] + [VMEM_SPEC] * 10,
+        in_specs=[pl.BlockSpec(memory_space=pltpu.SMEM)] + [VMEM_SPEC] * 17,
         out_specs=[VMEM_SPEC] * 8,
         scratch_shapes=[
-            pltpu.VMEM((width, 3 * lanes), BF),
+            pltpu.VMEM((3 * lanes, width), BF),
             pltpu.VMEM((lanes, width), BF),
+            pltpu.VMEM((1, 3 * lanes), F32),
             pltpu.VMEM((seqs, rows, width), F32),
             pltpu.VMEM((seqs, rows, 1), F32),
             pltpu.VMEM((seqs, 4, rows, width), BF),
@@ -680,67 +758,86 @@
         + group_scratch(seqs, rows, width)
         + [pltpu.SemaphoreType.DMA((3, seqs, 3))] * 4,
         compiler_params=pltpu.CompilerParams(
-            collective_id=1, has_side_effects=True, vmem_limit_bytes=VMEM_BYTES
+            collective_id=0, has_side_effects=True, vmem_limit_bytes=VMEM_BYTES
         ),
         name="front",
     )(
-        lengths, frames, cotangent, query_weight, key_weight, value_weight, projection_bias,
-        out_weight, up_weight, down_weight, vectors,
+        lengths, frames, cotangent, query_rows, key_rows, value_rows, query_bias, value_bias,
+        out_weight, out_bias, first_gain, first_shift, up_weight, up_bias,
+        down_weight, down_bias, second_gain, second_shift,
     )
-    input_grad, wide_grad, out_grad, rear_sums = pl.pallas_call(
-        rear,
-        out_shape=[
-            shape(frames.shape, F32),
-            shape((width, 3 * lanes), F32),
-            shape((lanes, width), F32),
-            shape((1, 3 * lanes), F32),
-        ],
-        in_specs=[VMEM_SPEC] * 8,
-        out_specs=[VMEM_SPEC] * 4,
+    count = lax.axis_size("dp")
+    ringed = count % 2 == 0 and count & (count - 1) == 0 and width % (32 * count) == 0
+    half = width // (2 * count)
+    levels = 2 + count.bit_length() - 1
+    grads = [shape((count, 2, half, width), BF)] * 3 if ringed else [shape((4 * heads_width, width), F32)]
+    outs = pl.pallas_call(
+        functools.partial(rear, count if ringed else 0),
+        out_shape=[shape(frames.shape, F32)] + grads + [shape((8, width), F32)],
+        in_specs=[VMEM_SPEC] * 8 + [VMEM_SPEC if ringed else ANY_SPEC] * 2 + [VMEM_SPEC],
+        out_specs=[VMEM_SPEC] + [ANY_SPEC if ringed else VMEM_SPEC] * len(grads) + [VMEM_SPEC],
         scratch_shapes=[
-            pltpu.VMEM((width, 3 * lanes), BF),
+            pltpu.VMEM((3 * lanes, width), BF),
             pltpu.VMEM((lanes, width), BF),
             pltpu.VMEM((seqs, 4, rows, width), BF),
             pltpu.VMEM((length, lanes), BF),
-            pltpu.VMEM((seqs, length, 3 * lanes), BF),
+            pltpu.VMEM((length, 3 * lanes), BF),
             pltpu.VMEM((length, 3 * lanes), F32),
         ]
         + group_scratch(seqs, rows, width)
-        + [pltpu.SemaphoreType.DMA((seqs, 3))] * 4,
+        + [pltpu.SemaphoreType.DMA((seqs, 3))] * 4
+        + (
+            [
+                pltpu.VMEM((4 * heads_width, width), F32),
+                pltpu.VMEM((3, 2, half, width), BF),
+                pltpu.VMEM((3, 2, count - 1, half, width), BF),
+                pltpu.VMEM((3, count, 2, half, width), BF),
+            ]
+            + [pltpu.SemaphoreType.DMA((3, 2, count - 1))] * 4
+            + [pltpu.SemaphoreType.DMA((3,))]
+            + [pltpu.VMEM((levels, 8, width), F32)] * 2
+            + [pltpu.SemaphoreType.DMA((levels,))] * 2
+            if ringed
+            else []
+        ),
         compiler_params=pltpu.CompilerParams(
-            collective_id=2, has_side_effects=True, vmem_limit_bytes=VMEM_BYTES
+            collective_id=1, has_side_effects=True, vmem_limit_bytes=VMEM_BYTES
         ),
         name="rear",
     )(
-        grad_attended, full_frames, projected, context, query_weight, key_weight, value_weight, out_weight,
+        grad_attended, full_frames, projected, context, query_rows, key_rows, value_rows, out_weight,
+        up_grad, down_grad, sums,
     )
-    count = lax.axis_size("dp")
-    large = [wide_grad, out_grad, up_grad, down_grad]
-    if count % 2 == 0 and all(grad.shape[0] % (16 * count) == 0 for grad in large):
-        large = ring_sum(large, count)
+    input_grad, sums = outs[0], outs[-1]
+    if ringed:
+        up_grad, down_grad, heads_grad = (
+            grad.reshape(width, width).astype(F32) for grad in outs[1:4]
+        )
     else:
-        large = lax.psum(large, "dp")
-    wide_grad, out_grad, up_grad, down_grad = large
-    rear_sums, up_bias_grad = lax.psum((rear_sums[0], sums[6]), "dp")
-    small = lax.psum(sums[:6], ("dp", "tensor"))
+        up_grad, down_grad, heads_grad = lax.psum((up_grad, down_grad, outs[1]), "dp")
+        sums = lax.psum(sums, "dp")
+        sums = jnp.concatenate([lax.psum(sums[:6], "tensor"), sums[6:]])
+    query_grad, key_grad, value_grad, out_grad = (
+        heads_grad[index * heads_width : (index + 1) * heads_width] for index in range(4)
+    )
     return (
         layer_output,
         input_grad,
-        wide_grad[:, :heads_width],
-        rear_sums[:heads_width],
-        wide_grad[:, lanes : lanes + heads_width],
-        wide_grad[:, 2 * lanes : 2 * lanes + heads_width],
-        rear_sums[2 * lanes : 2 * lanes + heads_width],
-        out_grad[:heads_width],
-        small[5],
-        small[3],
-        small[4],
+        query_grad.T,
+        sums[7, :heads_width],
+        key_grad.T,
+        value_grad.T,
+        sums[7, 2 * lanes : 2 * lanes + heads_width],
+        out_grad,
+        sums[5],
+        sums[3],
+        sums[4],
         up_grad,
-        up_bias_grad,
+        sums[6],
         down_grad,
-        small[2],
-        small[0],
-        small[1],
+        sums[2],
+        sums[0],
+        sums[1],
     )
 
 

time: 327 us -> 239 us (0.73)
  blocking collectives: 57.6 us -> 0 us
  Pallas kernels: 243 us -> 227 us
  local copies, waits for them, and re-layouts: 19 us -> 8.49 us
    psum x2 -> x0, blocking collectives: 57.6 us -> none  [the longest x1 37 us: shards(): small = lax.psum(sums[:6], ('dp', 'tensor'))]
    pallas_call x2 -> x1, Pallas kernels: 141 us -> 124 us  [shards(): pl.pallas_call(functools.partial(rear, count if ringed else 0), out_shape...]
    unnamed x20 -> x10, local copies, waits for them, and re-layouts: 10.7 us -> 2.55 us
    another operation x8 -> x0, local copies, waits for them, and re-layouts: 5.47 us -> none  [shards(): jnp.stack([out_bias, first_gain, first_shift, down_bias, second_gain, sec...]
    slice x5 -> x3, local copies, waits for them, and re-layouts: 1.43 us -> 5.95 us  [the longest x1 2.82 us: shards(): heads_grad[index * heads_width:(index + 1) * heads_width]]
where the time goes in v3:
time: 239 us
  Pallas kernels  227 us (95%)
  local copies, waits for them, and re-layouts  8.49 us (4%)
  other arithmetic  2.7 us (1%)
    pallas_call x1, Pallas kernels, shards(): pl.pallas_call(functools.partial(rear, count if ringed else 0), out_shape...  124 us
    pallas_call x1, Pallas kernels, shards(): pl.pallas_call(front, out_shape=[shape(frames.shape, BF), shape((seqs, 4,...  103 us

profile of v3, /device:TPU:0, one launch (start us, length us, event | category | flops | bytes accessed | tf_op | source)
XLA Modules:
  0.0 239.1 jit_solution(9247263466141318832)
XLA Ops:
  0.7 103.4 %front.1 = (bf16[2,200,768]{2,1,0:T(8,128)(2,1)}, bf16[2,4,208,768]{3,2,1,0:T(8,128)(2,1)}, bf16[2,832,768]{2,1,0:T(8,128)(2,1)}, bf16[2,832,256]{2,1,0:T(8,128)...) custom-call(s32[2]{0:T(128)} %lengths.1, ...), custom_call_target="tpu_custom_call" | custom-call | tf_op jit(solution)/shard_map/front/pallas_call | solution.py:731
  104.0 123.8 %rear.1 = (f32[2,200,768]{2,1,0:T(8,128)}, bf16[8,2,48,768]{3,2,1,0:T(8,128)(2,1)}, bf16[8,2,48,768]{3,2,1,0:T(8,128)(2,1)}, bf16[8,2,48,768]{3,2,1,0:T(8,128)(2,1)}, f32[8,768]{1,0:T(8,128)}) custom-call(f32[2,208,768]{2,1,0:T(8,128)} %get-tuple-element.31.attended_in, bf16[2,4,208,768]{3,2,1,0:T(8,128)(2,1)} %get-tuple-element.32.full_frames, ...), custom_call_target="tpu_custom_call" | custom-call | tf_op jit(solution)/shard_map/rear/pallas_call | solution.py:774
  227.9 1.3 fusion.1
  229.2 1.8 slice_reduce_fusion
  231.0 0.0 copy-start.1
  231.0 0.0 copy-start.2
  231.0 2.8 %fusion = (f32[2,2,48,768]{3,2,1,0:T(8,128)}, f32[2,2,48,768]{3,2,1,0:T(8,128)}, f32[2,2,48,768]{3,2,1,0:T(8,128)}, f32[2,2,48,768]{3,2,1,0:T(8,128)}) fusion(bf16[8,2,48,768]{3,2,1,0:T(8,128)(2,1)} %get-tuple-element.39), kind=kLoop, calls=%fused_computation.9 | loop fusion | bytes 4718592 | tf_op jit(solution)/shard_map/slice | solution.py:821
  233.8 0.0 copy-done.1
  233.8 0.0 copy-done.2
  233.9 0.0 copy-start.3
  233.9 2.7 %bitcast_convert_fusion = (f32[768,768]{1,0:T(8,128)}, f32[768,768]{1,0:T(8,128)}) fusion(bf16[8,2,48,768]{3,2,1,0:T(8,128)(2,1)S(1)} %copy-done.2, bf16[8,2,48,768]{3,2,1,0:T(8,128)(2,1)S(1)} %copy-done.1), kind=kLoop, calls=%fused_computation | loop fusion | flops 1179648 | bytes 7077888 | tf_op jit(solution)/shard_map/convert_element_type | solution.py:814
  236.6 0.0 copy-start
  236.6 0.0 copy-done.3
  236.6 0.8 copy.37
  237.4 0.7 copy-done
  238.1 1.0 copy.38
Async XLA Ops:
  231.0 2.8 %copy-start.1 = (bf16[8,2,48,768]{3,2,1,0:T(8,128)(2,1)S(1)}, bf16[8,2,48,768]{3,2,1,0:T(8,128)(2,1)}, u32[]{:S(2)}) copy-start(bf16[8,2,48,768]{3,2,1,0:T(8,128)(2,1)} %get-tuple-element.41) | copy-start | bytes 3538948
  231.0 2.8 %copy-start.2 = (bf16[8,2,48,768]{3,2,1,0:T(8,128)(2,1)S(1)}, bf16[8,2,48,768]{3,2,1,0:T(8,128)(2,1)}, u32[]{:S(2)}) copy-start(bf16[8,2,48,768]{3,2,1,0:T(8,128)(2,1)} %get-tuple-element.42) | copy-start | bytes 3538948
  233.9 2.7 %copy-start.3 = (bf16[2,200,768]{2,1,0:T(8,128)(2,1)S(1)}, bf16[2,200,768]{2,1,0:T(8,128)(2,1)}, u32[]{:S(2)}) copy-start(bf16[2,200,768]{2,1,0:T(8,128)(2,1)} %get-tuple-element.75) | copy-start | bytes 1843204
  236.6 1.5 copy-start
